TPU v7x, 128 devices: a whole 4x4x4 slice. The times are simulated.
128 devices in a mesh: outer: 8 (over z, core), inner: 16 (over x, y).
Axes of the slice: x: 4, y: 4, z: 4, core: 2. Of those that a mesh axis runs over, the one named last changes fastest.
Arguments:
- queries: bfloat16 [131072, 2048], P(('outer', 'inner')), may hold values from -6 to 6
- key_rows: bfloat16 [131072, 2048], P(('outer', 'inner')), may hold values from -6 to 6
- value_rows: bfloat16 [131072, 2048], P(('outer', 'inner')), may hold values from -6 to 6
- norm_gain: float32 [2048], replicated, may hold values from 0.5 to 1.5
Outputs:
- mixed: bfloat16 [131072, 2048], P(('outer', 'inner'))
- final_state: float32 [131072], P(('outer', 'inner'))
All inputs are finite; a program needn't handle non-finite values.
Results may differ from a plain program's by a relative error of at most 0.005.
Values sent between devices are 32-bit elements; how exact they have to be, the bound alone decides.
No kernel may reach another device: no remote copies, remote signals or barrier semaphores. Data moves between devices by JAX's collectives and lax.ppermute only.
A program may use at most 256 MiB of HBM per device.

v0:
```python
import jax
import jax.numpy as jnp
from jax import lax
from jax.sharding import PartitionSpec as P

D = 2048
HEADS = 32
DK = 64
BLOCK = 128


def carried_in(array, axis, combine, identity):
    length, here = (lax.axis_size(axis), lax.axis_index(axis))
    everything = lax.all_gather(array, axis)
    start = jnp.broadcast_to(jnp.asarray(identity, array.dtype), array.shape)

    def turn(k, before):
        reached = k < here
        new = combine(before, everything[k])
        return jnp.where(reached, new, before)

    return lax.fori_loop(0, length, turn, start)


def from_root(array, axis, root):
    mine = lax.axis_index(axis) == root
    return lax.psum(jnp.where(mine, array, jnp.zeros_like(array)), axis)


def combine_add(earlier, later):
    return earlier + later


def shards(queries, key_rows, value_rows, norm_gain):
    local_rows = queries.shape[0]
    blocks = local_rows // BLOCK
    query_grid = queries.reshape(blocks, BLOCK, HEADS, DK)
    key_grid = key_rows.reshape(blocks, BLOCK, HEADS, DK)
    value_grid = value_rows.reshape(blocks, BLOCK, HEADS, DK)
    block_states = jnp.einsum(
        "nkhd,nkhe->nhde", key_grid, value_grid, preferred_element_type=jnp.float32
    )
    later_index = lax.broadcasted_iota(jnp.int32, (blocks, blocks), 0)
    earlier_index = lax.broadcasted_iota(jnp.int32, (blocks, blocks), 1)
    lower = (earlier_index < later_index).astype(jnp.float32)
    flat_states = block_states.reshape(blocks, HEADS * DK * DK)
    before_block = jnp.dot(
        lower, flat_states, precision=lax.Precision.HIGHEST, preferred_element_type=jnp.float32
    ).reshape(blocks, HEADS, DK, DK)
    own_total = jnp.sum(flat_states, axis=0).reshape(HEADS, DK * DK)
    zero_state = jnp.zeros_like(own_total)
    causal = jnp.tril(jnp.ones((BLOCK, BLOCK), jnp.float32))
    scores = (
        jnp.einsum("nqhd,nkhd->nhqk", query_grid, key_grid, preferred_element_type=jnp.float32)
        * causal
    )
    weights = scores.astype(jnp.bfloat16)
    inside = jnp.einsum("nhqk,nkhe->nqhe", weights, value_grid, preferred_element_type=jnp.float32)
    prefix = carried_in(own_total, ("outer", "inner"), combine_add, zero_state)
    devices = lax.axis_size("outer") * lax.axis_size("inner")
    share = HEADS * DK * DK // devices
    scale_total = float(local_rows * devices) ** (-0.5)
    last_state = from_root(
        (prefix + own_total).reshape(HEADS * DK * DK), ("outer", "inner"), devices - 1
    )
    rank = lax.axis_index("outer") * lax.axis_size("inner") + lax.axis_index("inner")
    own_share = lax.dynamic_slice_in_dim(last_state, rank * share, share, 0)
    final_state = own_share * scale_total
    states = (prefix.reshape(1, HEADS, DK, DK) + before_block).astype(jnp.bfloat16)
    carried = jnp.einsum("nqhd,nhde->nqhe", query_grid, states, preferred_element_type=jnp.float32)
    attended = carried + inside
    gain_grid = norm_gain.reshape(HEADS, DK)
    scaled = (
        attended
        * lax.rsqrt(jnp.mean(attended * attended, axis=-1, keepdims=True) + 1e-06)
        * gain_grid
    )
    mixed = scaled.reshape(local_rows, D).astype(jnp.bfloat16)
    return (mixed, final_state)


def solution(mesh):
    return jax.shard_map(
        shards,
        mesh=mesh,
        in_specs=(
            P(("outer", "inner"), None),
            P(("outer", "inner"), None),
            P(("outer", "inner"), None),
            P(),
        ),
        out_specs=(P(("outer", "inner"), None), P(("outer", "inner"))),
        check_vma=False,
    )
```

profile of v0, /device:TPU:1, one launch (start us, length us, event | category | flops | bytes accessed | tf_op | source)
XLA Modules:
  0.0 548.3 jit_solution(6453652981230500022)
XLA Ops:
  7.2 12.9 %reshape.56 = bf16[8,128,32,64]{3,2,1,0:T(8,128)(2,1)} reshape(bf16[1024,2048]{1,0:T(8,128)(2,1)} %param.7) | data formatting | bytes 8388608 | tf_op jit(solution)/shard_map/reshape | solution.py:38
  20.1 11.5 %copy.35 = bf16[8,128,32,64]{1,3,2,0:T(8,128)(2,1)} copy(bf16[8,128,32,64]{3,2,1,0:T(8,128)(2,1)} %reshape.56) | data formatting | bytes 8388608 | tf_op jit(solution)/shard_map/reshape | solution.py:38
  31.6 12.9 %reshape.57 = bf16[8,128,32,64]{3,2,1,0:T(8,128)(2,1)} reshape(bf16[1024,2048]{1,0:T(8,128)(2,1)} %param.8) | data formatting | bytes 8388608 | tf_op jit(solution)/shard_map/reshape | solution.py:39
  44.4 11.5 %copy.36 = bf16[8,128,32,64]{1,3,2,0:T(8,128)(2,1)} copy(bf16[8,128,32,64]{3,2,1,0:T(8,128)(2,1)} %reshape.57) | data formatting | bytes 8388608 | tf_op jit(solution)/shard_map/reshape | solution.py:39
  55.9 9.0 %fusion.10 = (f32[32,64,64]{2,1,0:T(8,128)S(1)}, f32[8,32,64,64]{3,2,1,0:T(8,128)}) fusion(bf16[8,128,32,64]{1,3,2,0:T(8,128)(2,1)} %copy.35, bf16[8,128,32,64]{1,3,2,0:T(8,128)(2,1)} %copy.36), kind=kOutput, calls=%fused_computation.18 | convolution fusion | flops 269352960 | bytes 13107200 | tf_op jit(solution)/shard_map/nkhd,nkhe->nhde/dot_general | solution.py:40
  66.9 12.9 %reshape.58 = bf16[8,128,32,64]{3,2,1,0:T(8,128)(2,1)} reshape(bf16[1024,2048]{1,0:T(8,128)(2,1)} %param.6) | data formatting | bytes 8388608 | tf_op jit(solution)/shard_map/reshape | solution.py:37
  79.7 11.6 %copy.40 = bf16[8,128,32,64]{1,3,2,0:T(8,128)(2,1)} copy(bf16[8,128,32,64]{3,2,1,0:T(8,128)(2,1)} %reshape.58) | data formatting | bytes 8388608 | tf_op jit(solution)/shard_map/reshape | solution.py:37
  91.3 7.7 %reshape.51 = f32[8,131072]{1,0:T(8,128)} reshape(f32[8,32,64,64]{3,2,1,0:T(8,128)} %get-tuple-element.112) | data formatting | bytes 8388608 | tf_op jit(solution)/shard_map/reshape | solution.py:46
  99.0 8.7 %dot_general.21 = f32[32,64,64,8]{2,1,0,3:T(8,128)} reshape(f32[131072,8]{0,1:T(8,128)} %bitcast.37) | data formatting | bytes 8388608 | tf_op jit(solution)/shard_map/dot_general | solution.py:47
  107.7 126.6 %all-gather.2.cloned.1.call-done = f32[128,32,4096]{2,1,0:T(8,128)} async-done(((f32[1,32,4096]{2,1,0:T(8,128)}), f32[128,32,4096]{2,1,0:T(8,128)}) %all-gather.2.cloned.1.call-update) | async-done | bytes 67108880 | tf_op jit(solution)/shard_map/all_gather | solution.py:14
  234.3 158.9 %while.14 = (s32[]{:T(128)}, f32[32,4096]{1,0:T(8,128)S(1)}, s32[]{:T(128)}, f32[128,32,4096]{2,1,0:T(8,128)}, s32[]{:T(128)}, /*index=5*/s32[]{:T(128)}) while((s32[]{:T(128)}, f32[32,4096]{1,0:T(8,128)S(1)}, s32[]{:T(128)}, f32[128,32,4096]{2,1,0:T(8,128)}, s32[]{:T(128)}, /*index=5*/s32[]{:T(128)}) %tuple.41), condition=%wide.region_2.3_spmd.clone, body=%wide.region_1.2_spmd.clone.sunk | while | flops 393220 | bytes 1572965 | solution.py:22
  235.6 1.2 add_select_fusion.2
  236.8 1.2 add_select_fusion.2
  238.1 1.2 add_select_fusion.2
  239.3 1.2 add_select_fusion.2
  240.5 1.2 add_select_fusion.2
  394.7 12.6 %add_convert_fusion = bf16[8,32,64,64]{3,0,2,1:T(8,128)(2,1)S(1)} fusion(f32[32,64,64]{2,1,0:T(8,128)S(1)} %add.66, f32[32,64,64,8]{2,1,0,3:T(8,128)} %dot_general.21), kind=kOutput, calls=%fused_computation.7 | convolution fusion | flops 102760512 | bytes 6815744 | tf_op jit(solution)/shard_map/dot_general | solution.py:47
  407.4 4.8 fusion.2
  412.1 14.9 %multiply_reduce_fusion = (f32[8,128,32]{1,2,0:T(8,128)S(1)}, f32[8,32,128,64]{2,3,1,0:T(8,128)}) fusion(f32[8,32,64,128]{3,2,1,0:T(8,128)} %fusion.2, bf16[8,128,32,64]{1,3,2,0:T(8,128)(2,1)} %copy.36, bf16[8,128,32,64]{1,3,2,0:T(8,128)(2,1)} %copy.40, bf16[8,128,32,64]{1,3,2,0:T(8,128)(2,1)} %copy.35, f32[128,128]{1,0:T(8,128)S(1)} %fusion.7), kind=kOutput, calls=%fused_computation.6 | convolution fusion | flops 1088389120 | bytes 29556736 | tf_op jit(solution)/shard_map/nhqk,nkhe->nqhe/dot_general | solution.py:58
  427.0 8.6 %multiply_convert_fusion.1 = bf16[8,128,32,64]{1,3,2,0:T(8,128)(2,1)} fusion(f32[32,64]{1,0:T(8,128)S(1)} %mul.49, f32[8,128,32]{1,2,0:T(8,128)S(1)} %add_rsqrt_fusion, f32[8,32,128,64]{2,3,1,0:T(8,128)} %get-tuple-element.114, f32[8,32,64,128]{3,2,1,0:T(8,128)} %fusion.2), kind=kLoop, calls=%fused_computation.5 | loop fusion | flops 8388608 | bytes 21110784 | tf_op jit(solution)/shard_map/convert_element_type | solution.py:78
  435.6 12.8 %copy.47 = bf16[8,128,32,64]{3,2,1,0:T(8,128)(2,1)} copy(bf16[8,128,32,64]{1,3,2,0:T(8,128)(2,1)} %multiply_convert_fusion.1) | data formatting | bytes 8388608
  448.4 12.3 %reshape.55 = bf16[1024,2048]{1,0:T(8,128)(2,1)} reshape(bf16[8,128,32,64]{3,2,1,0:T(8,128)(2,1)} %copy.47) | data formatting | bytes 8388608
  460.7 79.4 %all-reduce.2.cloned.1.call-done = f32[131072]{0:T(1024)} async-done(((f32[131072]{0:T(1024)}), f32[131072]{0:T(1024)}) %all-reduce.2.cloned.1.call-update) | async-done | bytes 524304 | tf_op jit(solution)/shard_map/psum | solution.py:27
  540.1 1.3 dynamic-slice_multiply_fusion
  (140 shorter events, 152.9 us)
Async XLA Ops:
  7.2 227.2 %all-gather.2.cloned.1.call-start = ((), (), s32[]{:S(2)}) async-start(), calls=%async_computation | async-start | bytes 67633152 | tf_op jit(solution)/shard_map/all_gather | solution.py:14
  55.9 10.8 %copy-start.1 = (f32[2048]{0:T(1024)S(1)}, f32[2048]{0:T(1024)}, u32[]{:S(2)}) copy-start(f32[2048]{0:T(1024)} %param.9) | copy-start | bytes 24580
  66.2 474.0 %all-reduce.2.cloned.1.call-start = ((), (), s32[]{:S(2)}) async-start(), calls=%async_computation.1 | async-start | bytes 1048576 | tf_op jit(solution)/shard_map/psum | solution.py:27
  394.7 12.6 %copy-start = (bf16[8,128,32,64]{1,3,2,0:T(8,128)(2,1)S(1)}, bf16[8,128,32,64]{1,3,2,0:T(8,128)(2,1)}, u32[]{:S(2)}) copy-start(bf16[8,128,32,64]{1,3,2,0:T(8,128)(2,1)} %copy.40) | copy-start | bytes 12582916
Sparse Core Ops, SparseCore 0:
  66.3 168.0 all-gather.1
  394.8 145.2 all-reduce.1
where the time goes:
time: 557 us; the launch traced here: 548 us
  waiting for transfers between devices  206 us (37%)
  other arithmetic  166 us (30%)
  local copies, waits for them, and re-layouts  118 us (21%)
  matrix products  41.3 us (7%)
  between operations  14.1 us (3%)
    select_n x128, other arithmetic, turn(): return jnp.where(reached, new, before)  156 us
    all_gather x1, waiting for transfers between devices, carried_in(): everything = lax.all_gather(array, axis)  127 us
    psum x1, waiting for transfers between devices, from_root(): return lax.psum(jnp.where(mine, array, jnp.zeros_like(array)), axis)  79.4 us
    unnamed x7, local copies, waits for them, and re-layouts  26.1 us
    reshape x2, local copies, waits for them, and re-layouts, shards(): query_grid = queries.reshape(blocks, BLOCK, HEADS, DK)  24.5 us
    reshape x2, local copies, waits for them, and re-layouts, shards(): value_grid = value_rows.reshape(blocks, BLOCK, HEADS, DK)  24.4 us
    reshape x2, local copies, waits for them, and re-layouts, shards(): key_grid = key_rows.reshape(blocks, BLOCK, HEADS, DK)  24.3 us
    dot_general x1, matrix products, shards(): jnp.einsum('nhqk,nkhe->nqhe', weights, value_grid, preferred_element_type...  14.9 us
  transfers between devices with their start and end apart: 2, of which 2 were waited for; matrix products, arithmetic and copies ran while one was open for 20% of the time, Pallas kernels for 0%

commit v1 on v0

v1 whole, which is shorter than its diff:
```python
import functools

import jax
import jax.numpy as jnp
from jax import lax
from jax.experimental import pallas as pl
from jax.experimental.pallas import tpu as pltpu
from jax.sharding import PartitionSpec as P


HEADS = 32
DK = 64
BLOCK = 128
LANES = 128
PAIRS = 16
ROWS = 1024
BLOCKS = ROWS // BLOCK
GROUPS = 4
GROUP_PAIRS = PAIRS // GROUPS
GROUP_COLS = GROUP_PAIRS * LANES
QUARTERS = 4
QROWS = DK // QUARTERS
AXES = ("outer", "inner")


def coordinates():
    outer, inner = lax.axis_index("outer"), lax.axis_index("inner")
    return outer // 2, outer % 2, inner // 4, inner % 4


def exchange(array, dz=0, dc=0, dx=0, dy=0):
    turn = ((dz * 2 + dc) * 4 + dx) * 4 + dy
    return lax.ppermute(array, AXES, [(rank, rank ^ turn) for rank in range(128)])


def on_chip(array):
    return pltpu.with_memory_space_constraint(array, pltpu.VMEM)


def off_chip(array):
    return pltpu.with_memory_space_constraint(array, pltpu.HBM)


def pair_state(key, value):
    full = lax.dot_general(
        key, value, (((0,), (0,)), ((), ())), preferred_element_type=jnp.float32
    )
    lane = lax.broadcasted_iota(jnp.int32, (DK, LANES), 1)
    return jnp.where(lane < DK, full[:DK], full[DK:])


def totals_kernel(k_hbm, v_hbm, total_ref, k_ref, v_ref, sems):
    copies = []
    for i in range(GROUPS):
        cols = pl.ds(i * GROUP_COLS, GROUP_COLS)
        pair = (
            pltpu.make_async_copy(k_hbm.at[:, cols], k_ref.at[:, cols], sems.at[0, i]),
            pltpu.make_async_copy(v_hbm.at[:, cols], v_ref.at[:, cols], sems.at[1, i]),
        )
        for copy in pair:
            copy.start()
        copies.append(pair)
    _, _, _, y = coordinates()
    for i in range(GROUPS):
        for copy in copies[i]:
            copy.wait()
        for j in range(GROUP_PAIRS):
            p = i * GROUP_PAIRS + j
            cols = pl.ds(p * LANES, LANES)
            state = pair_state(k_ref[:, cols], v_ref[:, cols])
            for c in range(QUARTERS):
                total_ref[y ^ c, p] = state[c * QROWS : (c + 1) * QROWS]


def totals(keys, values):
    return pl.pallas_call(
        totals_kernel,
        out_shape=(
            jax.ShapeDtypeStruct((QUARTERS, PAIRS, QROWS, LANES), jnp.float32),
            pltpu.VMEM((ROWS, HEADS * DK), jnp.bfloat16),
            pltpu.VMEM((ROWS, HEADS * DK), jnp.bfloat16),
        ),
        in_specs=[pl.BlockSpec(memory_space=pl.ANY)] * 2,
        out_specs=(pl.BlockSpec(memory_space=pltpu.VMEM),) * 3,
        scratch_shapes=[pltpu.SemaphoreType.DMA((2, GROUPS))],
        compiler_params=pltpu.CompilerParams(vmem_limit_bytes=12 << 20),
        name="totals",
    )(off_chip(keys), off_chip(values))


def inside_kernel(group, q_hbm, k_ref, v_ref, att_ref, before_ref, q_ref, run_ref, sem):
    start = group * GROUP_COLS
    copy = pltpu.make_async_copy(q_hbm.at[:, pl.ds(start, GROUP_COLS)], q_ref, sem)
    copy.start()
    run_ref[...] = jnp.zeros_like(run_ref)
    lane = lax.broadcasted_iota(jnp.int32, (BLOCK, LANES), 1)
    low = lane < DK
    row = lax.broadcasted_iota(jnp.int32, (BLOCK, 2 * BLOCK), 0)
    col = lax.broadcasted_iota(jnp.int32, (BLOCK, 2 * BLOCK), 1)
    causal = (col % BLOCK) <= row
    copy.wait()

    def block(b, _):
        rows = pl.ds(pl.multiple_of(b * BLOCK, BLOCK), BLOCK)
        for j in range(GROUP_PAIRS):
            here = pl.ds(j * LANES, LANES)
            cols = pl.ds(start + j * LANES, LANES)
            q, k, v = q_ref[rows, here], k_ref[rows, cols], v_ref[rows, cols]
            zero = jnp.zeros_like(k)
            k_both = jnp.concatenate([jnp.where(low, k, zero), jnp.where(low, zero, k)], 0)
            v_both = jnp.concatenate([jnp.where(low, v, zero), jnp.where(low, zero, v)], 0)
            scores = lax.dot_general(
                q, k_both, (((1,), (1,)), ((), ())), preferred_element_type=jnp.float32
            )
            weights = jnp.where(causal, scores, 0.0).astype(jnp.bfloat16)
            att_ref[rows, here] = jnp.dot(
                weights, v_both, preferred_element_type=jnp.float32
            )
            run = run_ref[j]
            before_ref[b, j] = run
            run_ref[j] = run + pair_state(k, v)
        return 0

    lax.fori_loop(0, BLOCKS, block, 0)


def inside(group, queries, keys, values):
    return pl.pallas_call(
        functools.partial(inside_kernel, group),
        out_shape=(
            pltpu.VMEM((ROWS, GROUP_COLS), jnp.float32),
            pltpu.VMEM((BLOCKS, GROUP_PAIRS, DK, LANES), jnp.float32),
            pltpu.VMEM((ROWS, GROUP_COLS), jnp.bfloat16),
        ),
        in_specs=[
            pl.BlockSpec(memory_space=pl.ANY),
            pl.BlockSpec(memory_space=pltpu.VMEM),
            pl.BlockSpec(memory_space=pltpu.VMEM),
        ],
        out_specs=(pl.BlockSpec(memory_space=pltpu.VMEM),) * 3,
        scratch_shapes=[
            pltpu.VMEM((GROUP_PAIRS, DK, LANES), jnp.float32),
            pltpu.SemaphoreType.DMA(()),
        ],
        compiler_params=pltpu.CompilerParams(vmem_limit_bytes=12 << 20),
        cost_estimate=pl.CostEstimate(
            flops=400_000_000, bytes_accessed=8 << 20, transcendentals=0
        ),
    )(off_chip(queries), on_chip(keys), on_chip(values))


def output_kernel(*refs):
    prefix_refs, refs = refs[:QUARTERS], refs[QUARTERS:]
    att_refs, refs = refs[:GROUPS], refs[GROUPS:]
    before_refs, refs = refs[:GROUPS], refs[GROUPS:]
    q_refs, refs = refs[:GROUPS], refs[GROUPS:]
    final_ref, gain_ref, mixed_hbm, final_out, prefix, stage, sems = refs
    _, _, x, y = coordinates()
    lane = lax.broadcasted_iota(jnp.int32, (8, LANES), 1)
    even, odd = final_ref[pl.ds(0, 8, stride=2)], final_ref[pl.ds(1, 8, stride=2)]
    first = jnp.where(lane < DK, even, pltpu.roll(odd, DK, 1))
    second = jnp.where(lane < DK, pltpu.roll(even, DK, 1), odd)
    final_out[...] = jnp.where(x % 2 == 0, first, second) * float(ROWS * 128) ** (-0.5)
    for c in range(QUARTERS):
        prefix[y ^ c] = prefix_refs[c][...]
    wide = 2 * LANES
    owner_row = lax.broadcasted_iota(jnp.int32, (wide, wide), 0) // DK
    owner_col = lax.broadcasted_iota(jnp.int32, (wide, wide), 1) // DK
    average = jnp.where(owner_row == owner_col, 1.0 / DK, 0.0).astype(jnp.bfloat16)
    lane = lax.broadcasted_iota(jnp.int32, (DK, LANES), 1)
    low = lane < DK
    nothing = jnp.zeros((LANES, LANES), jnp.bfloat16)

    def out_copy(b, slot):
        rows = pl.ds(pl.multiple_of(b * BLOCK, BLOCK), BLOCK)
        return pltpu.make_async_copy(stage.at[slot], mixed_hbm.at[rows], sems.at[slot])

    def block(b, _):
        slot = b % 2
        rows = pl.ds(pl.multiple_of(b * BLOCK, BLOCK), BLOCK)

        @pl.when(b >= 2)
        def _():
            out_copy(b - 2, slot).wait()

        for quad in range(PAIRS // 2):
            group, inner = divmod(quad * 2, GROUP_PAIRS)
            halves = []
            for j in range(2):
                p = quad * 2 + j
                before = jnp.concatenate([prefix[c, p] for c in range(QUARTERS)], 0)
                state = (before + before_refs[group][b, inner + j]).astype(jnp.bfloat16)
                zero = jnp.zeros_like(state)
                halves.append(
                    jnp.concatenate(
                        [jnp.where(low, state, zero), jnp.where(low, zero, state)], 0
                    )
                )
            states = jnp.concatenate(
                [
                    jnp.concatenate([halves[0], nothing], 1),
                    jnp.concatenate([nothing, halves[1]], 1),
                ],
                0,
            )
            here = pl.ds(inner * LANES, wide)
            cols = pl.ds(quad * wide, wide)
            attended = att_refs[group][rows, here] + jnp.dot(
                q_refs[group][rows, here], states, preferred_element_type=jnp.float32
            )
            mean = jnp.dot(
                (attended * attended).astype(jnp.bfloat16),
                average,
                preferred_element_type=jnp.float32,
            )
            scaled = attended * lax.rsqrt(mean + 1e-06) * gain_ref[:, cols]
            stage[slot, :, cols] = scaled.astype(jnp.bfloat16)
        out_copy(b, slot).start()
        return 0

    lax.fori_loop(0, BLOCKS, block, 0)
    for b in (BLOCKS - 2, BLOCKS - 1):
        out_copy(b, b % 2).wait()


def output(prefixes, atts, befores, qs, final, gain):
    in_vmem = pl.BlockSpec(memory_space=pltpu.VMEM)
    return pl.pallas_call(
        output_kernel,
        out_shape=(
            jax.ShapeDtypeStruct((ROWS, HEADS * DK), jnp.bfloat16),
            jax.ShapeDtypeStruct((8, LANES), jnp.float32),
        ),
        in_specs=[in_vmem] * (4 * GROUPS + 2),
        out_specs=(pl.BlockSpec(memory_space=pl.ANY), in_vmem),
        scratch_shapes=[
            pltpu.VMEM((QUARTERS, PAIRS, QROWS, LANES), jnp.float32),
            pltpu.VMEM((2, BLOCK, HEADS * DK), jnp.bfloat16),
            pltpu.SemaphoreType.DMA((2,)),
        ],
        compiler_params=pltpu.CompilerParams(vmem_limit_bytes=12 << 20),
        name="output",
    )(*prefixes, *map(on_chip, (*atts, *befores, *qs)), final, gain)


def keep(condition, array):
    return jnp.where(condition, array, jnp.zeros_like(array))


def plane_kernel(row_ref, core_ref, *refs):
    z, core, x, _ = coordinates()
    column, (before_ref, final_ref, *send_refs) = refs[:3], refs[3:]
    row_sum, other_core = row_ref[...], core_ref[...]
    before = keep(core == 1, other_core)
    for k in range(1, 4):
        before = before + keep((z ^ k) < z, column[k - 1][...])
    before_ref[...] = before

    def final_pair(k):
        p = (z * 2 + core) * 2 + (x ^ k) // 2
        chip = row_ref[p] + core_ref[p]
        return chip + (column[0][p] + column[1][p] + column[2][p])

    final_ref[...] = final_pair(0)
    for k in range(1, 4):
        send_refs[k - 1][:PAIRS] = before + keep(x < (x ^ k), row_sum)
        send_refs[k - 1][PAIRS] = final_pair(k)


def prefix_kernel(before_ref, final_ref, *refs):
    _, _, _, y = coordinates()
    plane, ring, sums, final_out = refs[:3], refs[3:7], refs[7:11], refs[11]
    rows_before = before_ref[...] + (
        plane[0][:PAIRS] + plane[1][:PAIRS] + plane[2][:PAIRS]
    )
    states = [r[...] for r in ring]
    for j in range(4):
        shorter = rows_before
        for k in range(4):
            if k != j:
                shorter = shorter + keep((y ^ k) < (y ^ j), states[k])
        sums[j][...] = shorter
    final_out[...] = final_ref[...] + (
        plane[0][PAIRS] + plane[1][PAIRS] + plane[2][PAIRS]
    )


def small_call(kernel, out_shapes, *args):
    in_vmem = pl.BlockSpec(memory_space=pltpu.VMEM)
    return pl.pallas_call(
        kernel,
        out_shape=[jax.ShapeDtypeStruct(s, jnp.float32) for s in out_shapes],
        in_specs=[in_vmem] * len(args),
        out_specs=[in_vmem] * len(out_shapes),
        compiler_params=pltpu.CompilerParams(vmem_limit_bytes=4 << 20),
    )(*args)


def steps(queries, key_rows, value_rows, norm_gain):
    total, keys, values = totals(key_rows, value_rows)
    pieces = []
    for g in range(GROUPS):
        pieces.append(inside(g, queries, keys, values))
    atts, befores, qs = zip(*pieces)

    ring = [total[0]] + [exchange(total[k], dy=k) for k in range(1, 4)]
    row_sum = (ring[0] + ring[1]) + (ring[2] + ring[3])
    other_core = exchange(row_sum, dc=1)
    chip_sum = row_sum + other_core
    column = [exchange(chip_sum, dz=k) for k in range(1, 4)]
    quarter = (PAIRS, QROWS, LANES)
    pair = (QROWS, LANES)
    before, final, *sends = small_call(
        plane_kernel,
        [quarter, pair] + [(PAIRS + 1, QROWS, LANES)] * 3,
        row_sum,
        other_core,
        *column,
    )
    plane = [exchange(sends[k - 1], dx=k) for k in range(1, 4)]
    *sums, final = small_call(prefix_kernel, [quarter] * 4 + [pair], before, final, *plane, *ring)
    prefixes = [sums[0]] + [exchange(sums[k], dy=k) for k in range(1, 4)]
    mixed, final_state = output(
        prefixes, atts, befores, qs, final, norm_gain.reshape(1, HEADS * DK)
    )
    return (mixed, final_state.reshape(8 * LANES))


def solution(mesh):
    return jax.shard_map(
        steps,
        mesh=mesh,
        in_specs=(P(AXES, None), P(AXES, None), P(AXES, None), P()),
        out_specs=(P(AXES, None), P(AXES)),
        check_vma=False,
    )
```

time: 557 us -> 84.6 us (0.15); the launches traced: 548 us -> 83.6 us
  waiting for transfers between devices: 206 us -> 26.1 us
  other arithmetic: 166 us -> 0.05 us
  local copies, waits for them, and re-layouts: 118 us -> 0.04 us
  matrix products: 41.3 us -> 0 us
  Pallas kernels: 0 us -> 37.7 us
  starting transfers between devices: 0.26 us -> 18.9 us
  between operations: 14.1 us -> 0.75 us
    select_n x129 -> x0, other arithmetic: 156 us -> none  [the longest x128 156 us: turn(): return jnp.where(reached, new, before)]
    all_gather x1 -> x0, waiting for transfers between devices: 127 us -> none  [carried_in(): everything = lax.all_gather(array, axis)]
    reshape x8 -> x0, local copies, waits for them, and re-layouts: 81.3 us -> none  [the longest x2 24.5 us: shards(): query_grid = queries.reshape(blocks, BLOCK, HEADS, DK)]
    psum x1 -> x0, waiting for transfers between devices: 79.4 us -> none  [from_root(): return lax.psum(jnp.where(mine, array, jnp.zeros_like(array)), axis)]
    dot_general x4 -> x0, matrix products: 41.3 us -> none  [the longest x1 14.9 us: shards(): jnp.einsum('nhqk,nkhe->nqhe', weights, value_grid, preferred_element_type...]
    pallas_call x0 -> x8, Pallas kernels: none -> 37.7 us  [the longest x4 26.6 us: inside(): pl.pallas_call(functools.partial(inside_kernel, group), out_shape=(pltpu....]
    unnamed x7 -> x2, local copies, waits for them, and re-layouts: 26.1 us -> 0.01 us
    ppermute x0 -> x13, waiting for transfers between devices: none -> 26.1 us  [exchange(): lax.ppermute(array, AXES, [(rank, rank ^ turn) for rank in range(128)])]
  transfers between devices with their start and end apart: 2 -> 13, of which waited for: 2 -> 10; matrix products, arithmetic and copies ran while one was open for 20% -> 0% of each run, Pallas kernels for 0% -> 32%
where the time goes in v1:
time: 84.6 us; the launch traced here: 83.6 us
  Pallas kernels  37.7 us (45%)
  waiting for transfers between devices  26.1 us (31%)
  starting transfers between devices  18.9 us (22%)
    pallas_call x4, Pallas kernels, inside(): pl.pallas_call(functools.partial(inside_kernel, group), out_shape=(pltpu....  26.6 us
    ppermute x13, waiting for transfers between devices, exchange(): lax.ppermute(array, AXES, [(rank, rank ^ turn) for rank in range(128)])  26.1 us
    ppermute x13, starting transfers between devices, exchange(): lax.ppermute(array, AXES, [(rank, rank ^ turn) for rank in range(128)])  18.9 us
    pallas_call x1, Pallas kernels, output(): pl.pallas_call(output_kernel, out_shape=(jax.ShapeDtypeStruct((ROWS, HEAD...  6.7 us
    pallas_call x1, Pallas kernels, totals(): pl.pallas_call(totals_kernel, out_shape=(jax.ShapeDtypeStruct((QUARTERS,...  4.15 us
  transfers between devices with their start and end apart: 13, of which 10 were waited for; matrix products, arithmetic and copies ran while one was open for 0% of the time, Pallas kernels for 32%

profile of v1, /device:TPU:1, one launch (start us, length us, event | category | flops | bytes accessed | tf_op | source)
XLA Modules:
  0.0 83.6 jit_solution(16862991666875503932)
XLA Ops:
  0.6 4.2 %totals.1 = (f32[4,16,16,128]{3,2,1,0:T(8,128)S(1)}, bf16[1024,2048]{1,0:T(8,128)(2,1)S(1)}, bf16[1024,2048]{1,0:T(8,128)(2,1)S(1)}) custom-call(bf16[1024,2048]{1,0:T(8,128)(2,1)} %k_hbm.1, bf16[1024,2048]{1,0:T(8,128)(2,1)} %v_hbm.1), custom_call_target="tpu_custom_call" | custom-call | tf_op jit(solution)/shard_map/totals/pallas_call | solution.py:76
  4.8 2.2 %collective-permute-start = (f32[16,16,128]{2,1,0:T(8,128)S(1)}, f32[16,16,128]{2,1,0:T(8,128)S(1)}, u32[]{:S(2)}, u32[]{:S(2)}) collective-permute-start(f32[16,16,128]{2,1,0:T(8,128)S(1)} %get-tuple-element.59), channel_id=1, source_target_pairs={{0,1},{1,0},{2,3},{3,2},{4,5},{5,4},{6,7},{7,6},{8,9},{9,8},{10,11... | collective-permute-start | bytes 393224 | tf_op jit(solution)/shard_map/ppermute | solution.py:33
  7.0 2.6 %collective-permute-start.1 = (f32[16,16,128]{2,1,0:T(8,128)S(1)}, f32[16,16,128]{2,1,0:T(8,128)S(1)}, u32[]{:S(2)}, u32[]{:S(2)}) collective-permute-start(f32[16,16,128]{2,1,0:T(8,128)S(1)} %get-tuple-element.58), channel_id=1, source_target_pairs={{0,2},{1,3},{2,0},{3,1},{4,6},{5,7},{6,4},{7,5},{8,10},{9,11},{10,... | collective-permute-start | bytes 393224 | tf_op jit(solution)/shard_map/ppermute | solution.py:33
  9.7 0.2 collective-permute-done.refs_4_
  9.9 5.5 %collective-permute-done.1.refs_5_ = f32[16,16,128]{2,1,0:T(8,128)S(1)} collective-permute-done((f32[16,16,128]{2,1,0:T(8,128)S(1)}, f32[16,16,128]{2,1,0:T(8,128)S(1)}, u32[]{:S(2)}, u32[]{:S(2)}) %collective-permute-start.1) | collective-permute-done | bytes 131104 | tf_op jit(solution)/shard_map/ppermute | solution.py:33
  15.4 2.6 %collective-permute-done.2.refs_6_ = f32[16,16,128]{2,1,0:T(8,128)S(1)} collective-permute-done((f32[16,16,128]{2,1,0:T(8,128)S(1)}, f32[16,16,128]{2,1,0:T(8,128)S(1)}, u32[]{:S(2)}, u32[]{:S(2)}) %collective-permute-start.2) | collective-permute-done | bytes 131104 | tf_op jit(solution)/shard_map/ppermute | solution.py:33
  18.0 1.2 %collective-permute-start.3 = (f32[16,16,128]{2,1,0:T(8,128)S(1)}, f32[16,16,128]{2,1,0:T(8,128)S(1)}, u32[]{:S(2)}, u32[]{:S(2)}) collective-permute-start(f32[16,16,128]{2,1,0:T(8,128)S(1)} %add_add_fusion.row_ref), channel_id=1, source_target_pairs={{0,16},{1,17},{2,18},{3,19},{4,20},{5,21},{6,22},{7,23},{8,24},{9,... | collective-permute-start | bytes 393224 | tf_op jit(solution)/shard_map/ppermute | solution.py:33
  19.2 1.0 %collective-permute-done.3.core_ref = f32[16,16,128]{2,1,0:T(8,128)S(1)} collective-permute-done((f32[16,16,128]{2,1,0:T(8,128)S(1)}, f32[16,16,128]{2,1,0:T(8,128)S(1)}, u32[]{:S(2)}, u32[]{:S(2)}) %collective-permute-start.3) | collective-permute-done | bytes 131104 | tf_op jit(solution)/shard_map/ppermute | solution.py:33
  20.2 1.7 %collective-permute-start.4 = (f32[16,16,128]{2,1,0:T(8,128)S(1)}, f32[16,16,128]{2,1,0:T(8,128)S(1)}, u32[]{:S(2)}, u32[]{:S(2)}) collective-permute-start(f32[16,16,128]{2,1,0:T(8,128)S(1)} %add.15), channel_id=1, source_target_pairs={{0,32},{1,33},{2,34},{3,35},{4,36},{5,37},{6,38},{7,39},{8,40},{9,... | collective-permute-start | bytes 393224 | tf_op jit(solution)/shard_map/ppermute | solution.py:33
  21.9 3.3 %collective-permute-start.5 = (f32[16,16,128]{2,1,0:T(8,128)S(1)}, f32[16,16,128]{2,1,0:T(8,128)S(1)}, u32[]{:S(2)}, u32[]{:S(2)}) collective-permute-start(f32[16,16,128]{2,1,0:T(8,128)S(1)} %add.15), channel_id=1, source_target_pairs={{0,64},{1,65},{2,66},{3,67},{4,68},{5,69},{6,70},{7,71},{8,72},{9,... | collective-permute-start | bytes 393224 | tf_op jit(solution)/shard_map/ppermute | solution.py:33
  25.3 6.0 %collective-permute-done.5.refs_1_ = f32[16,16,128]{2,1,0:T(8,128)S(1)} collective-permute-done((f32[16,16,128]{2,1,0:T(8,128)S(1)}, f32[16,16,128]{2,1,0:T(8,128)S(1)}, u32[]{:S(2)}, u32[]{:S(2)}) %collective-permute-start.5) | collective-permute-done | bytes 131104 | tf_op jit(solution)/shard_map/ppermute | solution.py:33
  31.3 2.5 %collective-permute-done.6.refs_2_ = f32[16,16,128]{2,1,0:T(8,128)S(1)} collective-permute-done((f32[16,16,128]{2,1,0:T(8,128)S(1)}, f32[16,16,128]{2,1,0:T(8,128)S(1)}, u32[]{:S(2)}, u32[]{:S(2)}) %collective-permute-start.6) | collective-permute-done | bytes 131104 | tf_op jit(solution)/shard_map/ppermute | solution.py:33
  33.9 1.3 %collective-permute-start.7 = (f32[17,16,128]{2,1,0:T(8,128)S(1)}, f32[17,16,128]{2,1,0:T(8,128)S(1)}, u32[]{:S(2)}, u32[]{:S(2)}) collective-permute-start(f32[17,16,128]{2,1,0:T(8,128)S(1)} %get-tuple-element.32), channel_id=1, source_target_pairs={{0,4},{1,5},{2,6},{3,7},{4,0},{5,1},{6,2},{7,3},{8,12},{9,13},{10,... | collective-permute-start | bytes 417800 | tf_op jit(solution)/shard_map/ppermute | solution.py:33
  35.2 2.5 %collective-permute-start.8 = (f32[17,16,128]{2,1,0:T(8,128)S(1)}, f32[17,16,128]{2,1,0:T(8,128)S(1)}, u32[]{:S(2)}, u32[]{:S(2)}) collective-permute-start(f32[17,16,128]{2,1,0:T(8,128)S(1)} %get-tuple-element.33), channel_id=1, source_target_pairs={{0,8},{1,9},{2,10},{3,11},{4,12},{5,13},{6,14},{7,15},{8,0},{9,1},... | collective-permute-start | bytes 417800 | tf_op jit(solution)/shard_map/ppermute | solution.py:33
  37.9 0.4 collective-permute-done.7.refs_0_
  38.3 5.2 %collective-permute-done.8.refs_1_ = f32[17,16,128]{2,1,0:T(8,128)S(1)} collective-permute-done((f32[17,16,128]{2,1,0:T(8,128)S(1)}, f32[17,16,128]{2,1,0:T(8,128)S(1)}, u32[]{:S(2)}, u32[]{:S(2)}) %collective-permute-start.8) | collective-permute-done | bytes 139296 | tf_op jit(solution)/shard_map/ppermute | solution.py:33
  43.5 2.6 %collective-permute-done.9.refs_2_ = f32[17,16,128]{2,1,0:T(8,128)S(1)} collective-permute-done((f32[17,16,128]{2,1,0:T(8,128)S(1)}, f32[17,16,128]{2,1,0:T(8,128)S(1)}, u32[]{:S(2)}, u32[]{:S(2)}) %collective-permute-start.9) | collective-permute-done | bytes 139296 | tf_op jit(solution)/shard_map/ppermute | solution.py:33
  46.3 1.5 %collective-permute-start.11 = (f32[16,16,128]{2,1,0:T(8,128)S(1)}, f32[16,16,128]{2,1,0:T(8,128)S(1)}, u32[]{:S(2)}, u32[]{:S(2)}) collective-permute-start(f32[16,16,128]{2,1,0:T(8,128)S(1)} %get-tuple-element.37), channel_id=1, source_target_pairs={{0,2},{1,3},{2,0},{3,1},{4,6},{5,7},{6,4},{7,5},{8,10},{9,11},{10,... | collective-permute-start | bytes 393224 | tf_op jit(solution)/shard_map/ppermute | solution.py:33
  47.7 2.4 %collective-permute-start.12 = (f32[16,16,128]{2,1,0:T(8,128)S(1)}, f32[16,16,128]{2,1,0:T(8,128)S(1)}, u32[]{:S(2)}, u32[]{:S(2)}) collective-permute-start(f32[16,16,128]{2,1,0:T(8,128)S(1)} %get-tuple-element.38), channel_id=1, source_target_pairs={{0,3},{1,2},{2,1},{3,0},{4,7},{5,6},{6,5},{7,4},{8,11},{9,10},{10,... | collective-permute-start | bytes 393224 | tf_op jit(solution)/shard_map/ppermute | solution.py:33
  50.1 6.7 %shard_map.63 = (f32[1024,512]{1,0:T(8,128)S(1)}, f32[8,4,64,128]{3,2,1,0:T(8,128)S(1)}, bf16[1024,512]{1,0:T(8,128)(2,1)S(1)}) custom-call(bf16[1024,2048]{1,0:T(8,128)(2,1)} %q_hbm.7, bf16[1024,2048]{1,0:T(8,128)(2,1)S(1)} %get-tuple-element.39.k_ref, bf16[1024,2048]{1,0:T(8,128)(2,1)S(1)} %get-tuple-element.40.v_ref), custom_call_target="tpu_custom_call" | custom-call | flops 400000000 | bytes 8388608 | tf_op jit(solution)/shard_map/pallas_call | solution.py:128
  56.8 6.7 %shard_map.64 = (f32[1024,512]{1,0:T(8,128)S(1)}, f32[8,4,64,128]{3,2,1,0:T(8,128)S(1)}, bf16[1024,512]{1,0:T(8,128)(2,1)S(1)}) custom-call(bf16[1024,2048]{1,0:T(8,128)(2,1)} %q_hbm.7, bf16[1024,2048]{1,0:T(8,128)(2,1)S(1)} %get-tuple-element.39.k_ref, bf16[1024,2048]{1,0:T(8,128)(2,1)S(1)} %get-tuple-element.40.v_ref), custom_call_target="tpu_custom_call" | custom-call | flops 400000000 | bytes 8388608 | tf_op jit(solution)/shard_map/pallas_call | solution.py:128
  63.5 6.7 %shard_map.62 = (f32[1024,512]{1,0:T(8,128)S(1)}, f32[8,4,64,128]{3,2,1,0:T(8,128)S(1)}, bf16[1024,512]{1,0:T(8,128)(2,1)S(1)}) custom-call(bf16[1024,2048]{1,0:T(8,128)(2,1)} %q_hbm.7, bf16[1024,2048]{1,0:T(8,128)(2,1)S(1)} %get-tuple-element.39.k_ref, bf16[1024,2048]{1,0:T(8,128)(2,1)S(1)} %get-tuple-element.40.v_ref), custom_call_target="tpu_custom_call" | custom-call | flops 400000000 | bytes 8388608 | tf_op jit(solution)/shard_map/pallas_call | solution.py:128
  70.2 6.7 %shard_map.61 = (f32[1024,512]{1,0:T(8,128)S(1)}, f32[8,4,64,128]{3,2,1,0:T(8,128)S(1)}, bf16[1024,512]{1,0:T(8,128)(2,1)S(1)}) custom-call(bf16[1024,2048]{1,0:T(8,128)(2,1)} %q_hbm.7, bf16[1024,2048]{1,0:T(8,128)(2,1)S(1)} %get-tuple-element.39.k_ref, bf16[1024,2048]{1,0:T(8,128)(2,1)S(1)} %get-tuple-element.40.v_ref), custom_call_target="tpu_custom_call" | custom-call | flops 400000000 | bytes 8388608 | tf_op jit(solution)/shard_map/pallas_call | solution.py:128
  76.9 6.7 %output.1 = (bf16[1024,2048]{1,0:T(8,128)(2,1)}, f32[8,128]{1,0:T(8,128)}) custom-call(f32[16,16,128]{2,1,0:T(8,128)S(1)} %get-tuple-element.35.refs_0_, f32[16,16,128]{2,1,0:T(8,128)S(1)} %collective-permute-done.10.refs_1_, f32[16,16,128]{2,1,0:T(8,128)S(1)} %collective-permute-done.11.refs_2_, f32[16,16,128]{2,1,0:T(8,128)S(1)} %collective-permute-done.12.refs_3_, ...), custom_call_target="tpu_custom_call" | custom-call | tf_op jit(solution)/shard_map/output/pallas_call | solution.py:228
  (15 shorter events, 0.7 us)
Async XLA Ops:
  4.8 5.1 %collective-permute-start = (f32[16,16,128]{2,1,0:T(8,128)S(1)}, f32[16,16,128]{2,1,0:T(8,128)S(1)}, u32[]{:S(2)}, u32[]{:S(2)}) collective-permute-start(f32[16,16,128]{2,1,0:T(8,128)S(1)} %get-tuple-element.59), channel_id=1, source_target_pairs={{0,1},{1,0},{2,3},{3,2},{4,5},{5,4},{6,7},{7,6},{8,9},{9,8},{10,11... | collective-permute-start | bytes 393224 | tf_op jit(solution)/shard_map/ppermute | solution.py:33
  7.0 8.3 %collective-permute-start.1 = (f32[16,16,128]{2,1,0:T(8,128)S(1)}, f32[16,16,128]{2,1,0:T(8,128)S(1)}, u32[]{:S(2)}, u32[]{:S(2)}) collective-permute-start(f32[16,16,128]{2,1,0:T(8,128)S(1)} %get-tuple-element.58), channel_id=1, source_target_pairs={{0,2},{1,3},{2,0},{3,1},{4,6},{5,7},{6,4},{7,5},{8,10},{9,11},{10,... | collective-permute-start | bytes 393224 | tf_op jit(solution)/shard_map/ppermute | solution.py:33
  9.6 8.3 %collective-permute-start.2 = (f32[16,16,128]{2,1,0:T(8,128)S(1)}, f32[16,16,128]{2,1,0:T(8,128)S(1)}, u32[]{:S(2)}, u32[]{:S(2)}) collective-permute-start(f32[16,16,128]{2,1,0:T(8,128)S(1)} %get-tuple-element.57), channel_id=1, source_target_pairs={{0,3},{1,2},{2,1},{3,0},{4,7},{5,6},{6,5},{7,4},{8,11},{9,10},{10,... | collective-permute-start | bytes 393224 | tf_op jit(solution)/shard_map/ppermute | solution.py:33
  18.0 2.2 %collective-permute-start.3 = (f32[16,16,128]{2,1,0:T(8,128)S(1)}, f32[16,16,128]{2,1,0:T(8,128)S(1)}, u32[]{:S(2)}, u32[]{:S(2)}) collective-permute-start(f32[16,16,128]{2,1,0:T(8,128)S(1)} %add_add_fusion.row_ref), channel_id=1, source_target_pairs={{0,16},{1,17},{2,18},{3,19},{4,20},{5,21},{6,22},{7,23},{8,24},{9,... | collective-permute-start | bytes 393224 | tf_op jit(solution)/shard_map/ppermute | solution.py:33
  20.2 5.1 %collective-permute-start.4 = (f32[16,16,128]{2,1,0:T(8,128)S(1)}, f32[16,16,128]{2,1,0:T(8,128)S(1)}, u32[]{:S(2)}, u32[]{:S(2)}) collective-permute-start(f32[16,16,128]{2,1,0:T(8,128)S(1)} %add.15), channel_id=1, source_target_pairs={{0,32},{1,33},{2,34},{3,35},{4,36},{5,37},{6,38},{7,39},{8,40},{9,... | collective-permute-start | bytes 393224 | tf_op jit(solution)/shard_map/ppermute | solution.py:33
  21.9 9.4 %collective-permute-start.5 = (f32[16,16,128]{2,1,0:T(8,128)S(1)}, f32[16,16,128]{2,1,0:T(8,128)S(1)}, u32[]{:S(2)}, u32[]{:S(2)}) collective-permute-start(f32[16,16,128]{2,1,0:T(8,128)S(1)} %add.15), channel_id=1, source_target_pairs={{0,64},{1,65},{2,66},{3,67},{4,68},{5,69},{6,70},{7,71},{8,72},{9,... | collective-permute-start | bytes 393224 | tf_op jit(solution)/shard_map/ppermute | solution.py:33
  25.2 8.6 %collective-permute-start.6 = (f32[16,16,128]{2,1,0:T(8,128)S(1)}, f32[16,16,128]{2,1,0:T(8,128)S(1)}, u32[]{:S(2)}, u32[]{:S(2)}) collective-permute-start(f32[16,16,128]{2,1,0:T(8,128)S(1)} %add.15), channel_id=1, source_target_pairs={{0,96},{1,97},{2,98},{3,99},{4,100},{5,101},{6,102},{7,103},{8,104... | collective-permute-start | bytes 393224 | tf_op jit(solution)/shard_map/ppermute | solution.py:33
  33.9 4.3 %collective-permute-start.7 = (f32[17,16,128]{2,1,0:T(8,128)S(1)}, f32[17,16,128]{2,1,0:T(8,128)S(1)}, u32[]{:S(2)}, u32[]{:S(2)}) collective-permute-start(f32[17,16,128]{2,1,0:T(8,128)S(1)} %get-tuple-element.32), channel_id=1, source_target_pairs={{0,4},{1,5},{2,6},{3,7},{4,0},{5,1},{6,2},{7,3},{8,12},{9,13},{10,... | collective-permute-start | bytes 417800 | tf_op jit(solution)/shard_map/ppermute | solution.py:33
  35.2 8.2 %collective-permute-start.8 = (f32[17,16,128]{2,1,0:T(8,128)S(1)}, f32[17,16,128]{2,1,0:T(8,128)S(1)}, u32[]{:S(2)}, u32[]{:S(2)}) collective-permute-start(f32[17,16,128]{2,1,0:T(8,128)S(1)} %get-tuple-element.33), channel_id=1, source_target_pairs={{0,8},{1,9},{2,10},{3,11},{4,12},{5,13},{6,14},{7,15},{8,0},{9,1},... | collective-permute-start | bytes 417800 | tf_op jit(solution)/shard_map/ppermute | solution.py:33
  37.7 8.4 %collective-permute-start.9 = (f32[17,16,128]{2,1,0:T(8,128)S(1)}, f32[17,16,128]{2,1,0:T(8,128)S(1)}, u32[]{:S(2)}, u32[]{:S(2)}) collective-permute-start(f32[17,16,128]{2,1,0:T(8,128)S(1)} %get-tuple-element.34), channel_id=1, source_target_pairs={{0,12},{1,13},{2,14},{3,15},{4,8},{5,9},{6,10},{7,11},{8,4},{9,5},... | collective-permute-start | bytes 417800 | tf_op jit(solution)/shard_map/ppermute | solution.py:33
  46.2 30.6 %collective-permute-start.10 = (f32[16,16,128]{2,1,0:T(8,128)S(1)}, f32[16,16,128]{2,1,0:T(8,128)S(1)}, u32[]{:S(2)}, u32[]{:S(2)}) collective-permute-start(f32[16,16,128]{2,1,0:T(8,128)S(1)} %get-tuple-element.36), channel_id=1, source_target_pairs={{0,1},{1,0},{2,3},{3,2},{4,5},{5,4},{6,7},{7,6},{8,9},{9,8},{10,11... | collective-permute-start | bytes 393224 | tf_op jit(solution)/shard_map/ppermute | solution.py:33
  46.3 30.6 %collective-permute-start.11 = (f32[16,16,128]{2,1,0:T(8,128)S(1)}, f32[16,16,128]{2,1,0:T(8,128)S(1)}, u32[]{:S(2)}, u32[]{:S(2)}) collective-permute-start(f32[16,16,128]{2,1,0:T(8,128)S(1)} %get-tuple-element.37), channel_id=1, source_target_pairs={{0,2},{1,3},{2,0},{3,1},{4,6},{5,7},{6,4},{7,5},{8,10},{9,11},{10,... | collective-permute-start | bytes 393224 | tf_op jit(solution)/shard_map/ppermute | solution.py:33
  47.7 29.1 %collective-permute-start.12 = (f32[16,16,128]{2,1,0:T(8,128)S(1)}, f32[16,16,128]{2,1,0:T(8,128)S(1)}, u32[]{:S(2)}, u32[]{:S(2)}) collective-permute-start(f32[16,16,128]{2,1,0:T(8,128)S(1)} %get-tuple-element.38), channel_id=1, source_target_pairs={{0,3},{1,2},{2,1},{3,0},{4,7},{5,6},{6,5},{7,4},{8,11},{9,10},{10,... | collective-permute-start | bytes 393224 | tf_op jit(solution)/shard_map/ppermute | solution.py:33
  70.1 6.7 %copy-start = (f32[2048]{0:T(1024)S(1)}, f32[2048]{0:T(1024)}, u32[]{:S(2)}) copy-start(f32[2048]{0:T(1024)} %param.7) | copy-start | bytes 24580

commit v2 on v1

v2 whole, which is shorter than its diff:
```python
import functools

import jax
import jax.numpy as jnp
from jax import lax
from jax.experimental import pallas as pl
from jax.experimental.pallas import tpu as pltpu
from jax.sharding import PartitionSpec as P


HEADS = 32
DK = 64
BLOCK = 128
LANES = 128
PAIRS = 16
ROWS = 1024
BLOCKS = ROWS // BLOCK
GROUPS = 4
GROUP_PAIRS = PAIRS // GROUPS
GROUP_COLS = GROUP_PAIRS * LANES
QUARTERS = 4
QROWS = DK // QUARTERS
WIDTH = HEADS * DK
AXES = ("outer", "inner")
IN_VMEM = pl.BlockSpec(memory_space=pltpu.VMEM)


def coordinates():
    outer, inner = lax.axis_index("outer"), lax.axis_index("inner")
    return outer // 2, outer % 2, inner // 4, inner % 4


def exchange(array, dz=0, dc=0, dx=0, dy=0):
    turn = ((dz * 2 + dc) * 4 + dx) * 4 + dy
    return lax.ppermute(array, AXES, [(rank, rank ^ turn) for rank in range(128)])


def on_chip(array):
    return pltpu.with_memory_space_constraint(array, pltpu.VMEM)


def off_chip(array):
    return pltpu.with_memory_space_constraint(array, pltpu.HBM)


def totals_kernel(k_hbm, v_hbm, total_ref, kt_ref, v_ref, k_ref, sems):
    copies = []
    for i in range(GROUPS):
        cols = pl.ds(i * GROUP_COLS, GROUP_COLS)
        pair = (
            pltpu.make_async_copy(k_hbm.at[:, cols], k_ref.at[:, cols], sems.at[0, i]),
            pltpu.make_async_copy(v_hbm.at[:, cols], v_ref.at[:, cols], sems.at[1, i]),
        )
        for copy in pair:
            copy.start()
        copies.append(pair)
    _, _, _, y = coordinates()
    low = lax.broadcasted_iota(jnp.int32, (DK, LANES), 1) < DK
    for i in range(GROUPS):
        for copy in copies[i]:
            copy.wait()
        for j in range(GROUP_PAIRS):
            p = i * GROUP_PAIRS + j
            cols = pl.ds(p * LANES, LANES)
            keys = k_ref[:, cols].T
            kt_ref[cols, :] = keys
            full = jnp.dot(keys, v_ref[:, cols], preferred_element_type=jnp.float32)
            state = jnp.where(low, full[:DK], full[DK:])
            for c in range(QUARTERS):
                total_ref[y ^ c, p] = state[c * QROWS : (c + 1) * QROWS]


def totals(keys, values):
    return pl.pallas_call(
        totals_kernel,
        out_shape=(
            jax.ShapeDtypeStruct((QUARTERS, PAIRS, QROWS, LANES), jnp.float32),
            pltpu.VMEM((WIDTH, ROWS), jnp.bfloat16),
            pltpu.VMEM((ROWS, WIDTH), jnp.bfloat16),
        ),
        in_specs=[pl.BlockSpec(memory_space=pl.ANY)] * 2,
        out_specs=(IN_VMEM,) * 3,
        scratch_shapes=[
            pltpu.VMEM((ROWS, WIDTH), jnp.bfloat16),
            pltpu.SemaphoreType.DMA((2, GROUPS)),
        ],
        compiler_params=pltpu.CompilerParams(vmem_limit_bytes=16 << 20),
        name="totals",
    )(off_chip(keys), off_chip(values))


def beside(state):
    low = lax.broadcasted_iota(jnp.int32, state.shape, 1) < DK
    zero = jnp.zeros_like(state)
    return jnp.concatenate([jnp.where(low, state, zero), jnp.where(low, zero, state)], 0)


def inside_kernel(group, *refs):
    q_hbm, refs = refs[0], refs[1:]
    q_ref = None
    if group > 0:
        q_ref, refs = refs[0], refs[1:]
    (kt_ref, v_ref, att_ref, before_ref), refs = refs[:4], refs[4:]
    start = group * GROUP_COLS
    *q_refs, mask_ref, sems = refs
    if group == 0:
        q_ref, q_refs = q_refs[0], q_refs[1:]
        own = pltpu.make_async_copy(q_hbm.at[:, pl.ds(0, GROUP_COLS)], q_ref, sems.at[0])
        own.start()
    if group < GROUPS - 1:
        ahead = pltpu.make_async_copy(
            q_hbm.at[:, pl.ds(start + GROUP_COLS, GROUP_COLS)], q_refs[0], sems.at[1]
        )
        ahead.start()
    row = lax.broadcasted_iota(jnp.int32, (BLOCK, 2 * BLOCK), 0)
    col = lax.broadcasted_iota(jnp.int32, (BLOCK, 2 * BLOCK), 1)
    mask_ref[...] = jnp.where((col % BLOCK) <= row, 1.0, 0.0).astype(jnp.bfloat16)
    half = jnp.zeros((DK, BLOCK), jnp.bfloat16)
    before = [jnp.zeros((DK, LANES), jnp.float32)] * GROUP_PAIRS
    if group == 0:
        own.wait()
    for b in range(BLOCKS):
        rows = pl.ds(b * BLOCK, BLOCK)
        last = b == BLOCKS - 1
        for j in range(GROUP_PAIRS):
            here = pl.ds(j * LANES, LANES)
            cols = pl.ds(start + j * LANES, LANES)
            q, keys, values = q_ref[rows, here], kt_ref[cols, rows], v_ref[rows, cols]
            first, second = keys[:DK], keys[DK:]
            k_both = jnp.concatenate(
                [
                    jnp.concatenate([first, half], 1),
                    jnp.concatenate([half, second], 1),
                ],
                0,
            )
            v_both = beside(values)
            scores = jnp.dot(q, k_both, preferred_element_type=jnp.float32)
            weights = scores.astype(jnp.bfloat16) * mask_ref[...]
            left = weights
            if not last:
                left = jnp.concatenate([weights, jnp.concatenate([first, second], 1)], 0)
            both = jnp.dot(left, v_both, preferred_element_type=jnp.float32)
            att_ref[rows, here] = both[:BLOCK]
            before_ref[b, j] = before[j]
            if not last:
                before[j] = before[j] + both[BLOCK:]
    if group < GROUPS - 1:
        ahead.wait()


def inside(group, queries, q_part, keys, values):
    part = pltpu.VMEM((ROWS, GROUP_COLS), jnp.bfloat16)
    fetched = (group == 0) + (group < GROUPS - 1)
    given = [] if q_part is None else [on_chip(q_part)]
    return pl.pallas_call(
        functools.partial(inside_kernel, group),
        out_shape=(
            pltpu.VMEM((ROWS, GROUP_COLS), jnp.float32),
            pltpu.VMEM((BLOCKS, GROUP_PAIRS, DK, LANES), jnp.float32),
        )
        + (part,) * fetched,
        in_specs=[pl.BlockSpec(memory_space=pl.ANY)] + [IN_VMEM] * (len(given) + 2),
        out_specs=(IN_VMEM,) * (2 + fetched),
        scratch_shapes=[
            pltpu.VMEM((BLOCK, 2 * BLOCK), jnp.bfloat16),
            pltpu.SemaphoreType.DMA((2,)),
        ],
        compiler_params=pltpu.CompilerParams(vmem_limit_bytes=10 << 20),
        cost_estimate=pl.CostEstimate(
            flops=400_000_000, bytes_accessed=8 << 20, transcendentals=0
        ),
    )(off_chip(queries), *given, on_chip(keys), on_chip(values))


def output_kernel(*refs):
    prefix_refs, refs = refs[:QUARTERS], refs[QUARTERS:]
    att_refs, refs = refs[:GROUPS], refs[GROUPS:]
    before_refs, refs = refs[:GROUPS], refs[GROUPS:]
    q_refs, refs = refs[:GROUPS], refs[GROUPS:]
    final_ref, gain_ref, mixed_hbm, final_out, prefix, stage, sems = refs
    _, _, x, y = coordinates()
    lane = lax.broadcasted_iota(jnp.int32, (8, LANES), 1)
    even, odd = final_ref[pl.ds(0, 8, stride=2)], final_ref[pl.ds(1, 8, stride=2)]
    first = jnp.where(lane < DK, even, pltpu.roll(odd, DK, 1))
    second = jnp.where(lane < DK, pltpu.roll(even, DK, 1), odd)
    final_out[...] = jnp.where(x % 2 == 0, first, second) * float(ROWS * 128) ** (-0.5)
    for c in range(QUARTERS):
        prefix[y ^ c] = prefix_refs[c][...]
    wide = 2 * LANES
    owner_row = lax.broadcasted_iota(jnp.int32, (wide, wide), 0) // DK
    owner_col = lax.broadcasted_iota(jnp.int32, (wide, wide), 1) // DK
    average = jnp.where(owner_row == owner_col, 1.0 / DK, 0.0).astype(jnp.bfloat16)
    nothing = jnp.zeros((LANES, LANES), jnp.bfloat16)
    copies = []
    for quad in range(PAIRS // 2):
        group, inner = divmod(quad * 2, GROUP_PAIRS)
        whole = [
            jnp.concatenate([prefix[c, quad * 2 + j] for c in range(QUARTERS)], 0)
            for j in range(2)
        ]
        here = pl.ds(inner * LANES, wide)
        cols = pl.ds(quad * wide, wide)
        parts = []
        for b in range(BLOCKS):
            rows = pl.ds(b * BLOCK, BLOCK)
            pair, other = (
                beside((whole[j] + before_refs[group][b, inner + j]).astype(jnp.bfloat16))
                for j in range(2)
            )
            states = jnp.concatenate(
                [
                    jnp.concatenate([pair, nothing], 1),
                    jnp.concatenate([nothing, other], 1),
                ],
                0,
            )
            carried = jnp.dot(
                q_refs[group][rows, here], states, preferred_element_type=jnp.float32
            )
            parts.append(att_refs[group][rows, here] + carried)
        attended = jnp.concatenate(parts, 0)
        mean = jnp.dot(
            (attended * attended).astype(jnp.bfloat16),
            average,
            preferred_element_type=jnp.float32,
        )
        scale = lax.rsqrt(mean + 1e-06) * gain_ref[:, cols]
        stage[:, cols] = (attended * scale).astype(jnp.bfloat16)
        copy = pltpu.make_async_copy(stage.at[:, cols], mixed_hbm.at[:, cols], sems.at[quad])
        copy.start()
        copies.append(copy)
    for copy in copies:
        copy.wait()


def output(prefixes, atts, befores, qs, final, gain):
    return pl.pallas_call(
        output_kernel,
        out_shape=(
            jax.ShapeDtypeStruct((ROWS, WIDTH), jnp.bfloat16),
            jax.ShapeDtypeStruct((8, LANES), jnp.float32),
        ),
        in_specs=[IN_VMEM] * (QUARTERS + 3 * GROUPS + 2),
        out_specs=(pl.BlockSpec(memory_space=pl.ANY), IN_VMEM),
        scratch_shapes=[
            pltpu.VMEM((QUARTERS, PAIRS, QROWS, LANES), jnp.float32),
            pltpu.VMEM((ROWS, WIDTH), jnp.bfloat16),
            pltpu.SemaphoreType.DMA((PAIRS // 2,)),
        ],
        compiler_params=pltpu.CompilerParams(vmem_limit_bytes=12 << 20),
        name="output",
    )(*prefixes, *map(on_chip, (*atts, *befores, *qs)), final, gain)


def keep(condition, array):
    return jnp.where(condition, array, jnp.zeros_like(array))


def plane_kernel(row_ref, core_ref, *refs):
    z, core, x, _ = coordinates()
    column, (before_ref, final_ref, *send_refs) = refs[:3], refs[3:]
    row_sum, other_core = row_ref[...], core_ref[...]
    before = keep(core == 1, other_core)
    for k in range(1, 4):
        before = before + keep((z ^ k) < z, column[k - 1][...])
    before_ref[...] = before

    def final_pair(k):
        p = (z * 2 + core) * 2 + (x ^ k) // 2
        chip = row_ref[p] + core_ref[p]
        return chip + (column[0][p] + column[1][p] + column[2][p])

    final_ref[...] = final_pair(0)
    for k in range(1, 4):
        send_refs[k - 1][:PAIRS] = before + keep(x < (x ^ k), row_sum)
        send_refs[k - 1][PAIRS] = final_pair(k)


def prefix_kernel(before_ref, final_ref, *refs):
    _, _, _, y = coordinates()
    plane, ring, sums, final_out = refs[:3], refs[3:7], refs[7:11], refs[11]
    rows_before = before_ref[...] + (
        plane[0][:PAIRS] + plane[1][:PAIRS] + plane[2][:PAIRS]
    )
    states = [r[...] for r in ring]
    for j in range(4):
        shorter = rows_before
        for k in range(4):
            if k != j:
                shorter = shorter + keep((y ^ k) < (y ^ j), states[k])
        sums[j][...] = shorter
    final_out[...] = final_ref[...] + (
        plane[0][PAIRS] + plane[1][PAIRS] + plane[2][PAIRS]
    )


def small_call(kernel, out_shapes, *args):
    return pl.pallas_call(
        kernel,
        out_shape=[jax.ShapeDtypeStruct(s, jnp.float32) for s in out_shapes],
        in_specs=[IN_VMEM] * len(args),
        out_specs=[IN_VMEM] * len(out_shapes),
        compiler_params=pltpu.CompilerParams(vmem_limit_bytes=4 << 20),
    )(*args)


def steps(queries, key_rows, value_rows, norm_gain):
    total, keys, values = totals(key_rows, value_rows)
    atts, befores, qs = [], [], []
    for g in range(GROUPS):
        attended, before, *fetched = inside(g, queries, qs[g] if g else None, keys, values)
        atts.append(attended)
        befores.append(before)
        qs.extend(fetched)

    ring = [total[0]] + [exchange(total[k], dy=k) for k in range(1, 4)]
    row_sum = (ring[0] + ring[1]) + (ring[2] + ring[3])
    other_core = exchange(row_sum, dc=1)
    chip_sum = row_sum + other_core
    column = [exchange(chip_sum, dz=k) for k in range(1, 4)]
    quarter = (PAIRS, QROWS, LANES)
    pair = (QROWS, LANES)
    before, final, *sends = small_call(
        plane_kernel,
        [quarter, pair] + [(PAIRS + 1, QROWS, LANES)] * 3,
        row_sum,
        other_core,
        *column,
    )
    plane = [exchange(sends[k - 1], dx=k) for k in range(1, 4)]
    *sums, final = small_call(prefix_kernel, [quarter] * 4 + [pair], before, final, *plane, *ring)
    prefixes = [sums[0]] + [exchange(sums[k], dy=k) for k in range(1, 4)]
    mixed, final_state = output(
        prefixes, atts, befores, qs, final, norm_gain.reshape(1, WIDTH)
    )
    return (mixed, final_state.reshape(8 * LANES))


def solution(mesh):
    return jax.shard_map(
        steps,
        mesh=mesh,
        in_specs=(P(AXES, None), P(AXES, None), P(AXES, None), P()),
        out_specs=(P(AXES, None), P(AXES)),
        check_vma=False,
    )
```

time: 84.6 us -> 63.6 us (0.75)
  the two profiles are of different devices: /device:TPU:1 before, /device:TPU:0 now
where the time goes in v2:
time: 63.6 us; the launch traced here: 63.5 us
  Pallas kernels  21.9 us (34%)
  waiting for transfers between devices  21.7 us (34%)
  starting transfers between devices  18.9 us (30%)
  between operations  0.91 us (1%)
    ppermute x13, waiting for transfers between devices, exchange(): lax.ppermute(array, AXES, [(rank, rank ^ turn) for rank in range(128)])  21.7 us
    ppermute x13, starting transfers between devices, exchange(): lax.ppermute(array, AXES, [(rank, rank ^ turn) for rank in range(128)])  18.9 us
    pallas_call x4, Pallas kernels, inside(): pl.pallas_call(functools.partial(inside_kernel, group), out_shape=(pltpu....  13.2 us
    pallas_call x1, Pallas kernels, output(): pl.pallas_call(output_kernel, out_shape=(jax.ShapeDtypeStruct((ROWS, WIDT...  4.25 us
    pallas_call x1, Pallas kernels, totals(): pl.pallas_call(totals_kernel, out_shape=(jax.ShapeDtypeStruct((QUARTERS,...  4.21 us
  transfers between devices with their start and end apart: 13, of which 8 were waited for; matrix products, arithmetic and copies ran while one was open for 0% of the time, Pallas kernels for 21%

profile of v2, /device:TPU:0, one launch (start us, length us, event | category | flops | bytes accessed | tf_op | source)
XLA Modules:
  0.0 63.5 jit_solution(803559633637161827)
XLA Ops:
  0.6 4.2 %totals.1 = (f32[4,16,16,128]{3,2,1,0:T(8,128)S(1)}, bf16[2048,1024]{1,0:T(8,128)(2,1)S(1)}, bf16[1024,2048]{1,0:T(8,128)(2,1)S(1)}) custom-call(bf16[1024,2048]{1,0:T(8,128)(2,1)} %k_hbm.1, bf16[1024,2048]{1,0:T(8,128)(2,1)} %v_hbm.1), custom_call_target="tpu_custom_call" | custom-call | tf_op jit(solution)/shard_map/totals/pallas_call | solution.py:74
  4.9 3.2 %collective-permute-start.2 = (f32[16,16,128]{2,1,0:T(8,128)S(1)}, f32[16,16,128]{2,1,0:T(8,128)S(1)}, u32[]{:S(2)}, u32[]{:S(2)}) collective-permute-start(f32[16,16,128]{2,1,0:T(8,128)S(1)} %get-tuple-element.57), channel_id=1, source_target_pairs={{0,3},{1,2},{2,1},{3,0},{4,7},{5,6},{6,5},{7,4},{8,11},{9,10},{10,... | collective-permute-start | bytes 393224 | tf_op jit(solution)/shard_map/ppermute | solution.py:35
  8.1 0.6 collective-permute-start.1
  9.1 4.6 %collective-permute-done.2.refs_6_ = f32[16,16,128]{2,1,0:T(8,128)S(1)} collective-permute-done((f32[16,16,128]{2,1,0:T(8,128)S(1)}, f32[16,16,128]{2,1,0:T(8,128)S(1)}, u32[]{:S(2)}, u32[]{:S(2)}) %collective-permute-start.2) | collective-permute-done | bytes 131104 | tf_op jit(solution)/shard_map/ppermute | solution.py:35
  13.7 2.3 %collective-permute-done.1.refs_5_ = f32[16,16,128]{2,1,0:T(8,128)S(1)} collective-permute-done((f32[16,16,128]{2,1,0:T(8,128)S(1)}, f32[16,16,128]{2,1,0:T(8,128)S(1)}, u32[]{:S(2)}, u32[]{:S(2)}) %collective-permute-start.1) | collective-permute-done | bytes 131104 | tf_op jit(solution)/shard_map/ppermute | solution.py:35
  16.1 1.3 %collective-permute-done.3.core_ref = f32[16,16,128]{2,1,0:T(8,128)S(1)} collective-permute-done((f32[16,16,128]{2,1,0:T(8,128)S(1)}, f32[16,16,128]{2,1,0:T(8,128)S(1)}, u32[]{:S(2)}, u32[]{:S(2)}) %collective-permute-start.3) | collective-permute-done | bytes 131104 | tf_op jit(solution)/shard_map/ppermute | solution.py:35
  17.5 4.1 %collective-permute-start.6 = (f32[16,16,128]{2,1,0:T(8,128)S(1)}, f32[16,16,128]{2,1,0:T(8,128)S(1)}, u32[]{:S(2)}, u32[]{:S(2)}) collective-permute-start(f32[16,16,128]{2,1,0:T(8,128)S(1)} %add.15), channel_id=1, source_target_pairs={{0,96},{1,97},{2,98},{3,99},{4,100},{5,101},{6,102},{7,103},{8,104... | collective-permute-start | bytes 393224 | tf_op jit(solution)/shard_map/ppermute | solution.py:35
  21.6 0.9 %collective-permute-start.4 = (f32[16,16,128]{2,1,0:T(8,128)S(1)}, f32[16,16,128]{2,1,0:T(8,128)S(1)}, u32[]{:S(2)}, u32[]{:S(2)}) collective-permute-start(f32[16,16,128]{2,1,0:T(8,128)S(1)} %add.15), channel_id=1, source_target_pairs={{0,32},{1,33},{2,34},{3,35},{4,36},{5,37},{6,38},{7,39},{8,40},{9,... | collective-permute-start | bytes 393224 | tf_op jit(solution)/shard_map/ppermute | solution.py:35
  22.5 4.9 %collective-permute-done.6.refs_2_ = f32[16,16,128]{2,1,0:T(8,128)S(1)} collective-permute-done((f32[16,16,128]{2,1,0:T(8,128)S(1)}, f32[16,16,128]{2,1,0:T(8,128)S(1)}, u32[]{:S(2)}, u32[]{:S(2)}) %collective-permute-start.6) | collective-permute-done | bytes 131104 | tf_op jit(solution)/shard_map/ppermute | solution.py:35
  27.4 2.0 %collective-permute-done.5.refs_1_ = f32[16,16,128]{2,1,0:T(8,128)S(1)} collective-permute-done((f32[16,16,128]{2,1,0:T(8,128)S(1)}, f32[16,16,128]{2,1,0:T(8,128)S(1)}, u32[]{:S(2)}, u32[]{:S(2)}) %collective-permute-start.5) | collective-permute-done | bytes 131104 | tf_op jit(solution)/shard_map/ppermute | solution.py:35
  29.5 1.6 %collective-permute-start.7 = (f32[17,16,128]{2,1,0:T(8,128)S(1)}, f32[17,16,128]{2,1,0:T(8,128)S(1)}, u32[]{:S(2)}, u32[]{:S(2)}) collective-permute-start(f32[17,16,128]{2,1,0:T(8,128)S(1)} %get-tuple-element.32), channel_id=1, source_target_pairs={{0,4},{1,5},{2,6},{3,7},{4,0},{5,1},{6,2},{7,3},{8,12},{9,13},{10,... | collective-permute-start | bytes 417800 | tf_op jit(solution)/shard_map/ppermute | solution.py:35
  31.1 2.7 %collective-permute-start.8 = (f32[17,16,128]{2,1,0:T(8,128)S(1)}, f32[17,16,128]{2,1,0:T(8,128)S(1)}, u32[]{:S(2)}, u32[]{:S(2)}) collective-permute-start(f32[17,16,128]{2,1,0:T(8,128)S(1)} %get-tuple-element.33), channel_id=1, source_target_pairs={{0,8},{1,9},{2,10},{3,11},{4,12},{5,13},{6,14},{7,15},{8,0},{9,1},... | collective-permute-start | bytes 417800 | tf_op jit(solution)/shard_map/ppermute | solution.py:35
  33.8 0.5 collective-permute-start.9
  34.3 1.8 %collective-permute-done.7.refs_0_ = f32[17,16,128]{2,1,0:T(8,128)S(1)} collective-permute-done((f32[17,16,128]{2,1,0:T(8,128)S(1)}, f32[17,16,128]{2,1,0:T(8,128)S(1)}, u32[]{:S(2)}, u32[]{:S(2)}) %collective-permute-start.7) | collective-permute-done | bytes 139296 | tf_op jit(solution)/shard_map/ppermute | solution.py:35
  36.1 3.1 %collective-permute-done.8.refs_1_ = f32[17,16,128]{2,1,0:T(8,128)S(1)} collective-permute-done((f32[17,16,128]{2,1,0:T(8,128)S(1)}, f32[17,16,128]{2,1,0:T(8,128)S(1)}, u32[]{:S(2)}, u32[]{:S(2)}) %collective-permute-start.8) | collective-permute-done | bytes 139296 | tf_op jit(solution)/shard_map/ppermute | solution.py:35
  39.2 1.6 %collective-permute-done.9.refs_2_ = f32[17,16,128]{2,1,0:T(8,128)S(1)} collective-permute-done((f32[17,16,128]{2,1,0:T(8,128)S(1)}, f32[17,16,128]{2,1,0:T(8,128)S(1)}, u32[]{:S(2)}, u32[]{:S(2)}) %collective-permute-start.9) | collective-permute-done | bytes 139296 | tf_op jit(solution)/shard_map/ppermute | solution.py:35
  41.0 0.7 %collective-permute-start.10 = (f32[16,16,128]{2,1,0:T(8,128)S(1)}, f32[16,16,128]{2,1,0:T(8,128)S(1)}, u32[]{:S(2)}, u32[]{:S(2)}) collective-permute-start(f32[16,16,128]{2,1,0:T(8,128)S(1)} %get-tuple-element.36), channel_id=1, source_target_pairs={{0,1},{1,0},{2,3},{3,2},{4,5},{5,4},{6,7},{7,6},{8,9},{9,8},{10,11... | collective-permute-start | bytes 393224 | tf_op jit(solution)/shard_map/ppermute | solution.py:35
  41.7 2.9 %collective-permute-start.11 = (f32[16,16,128]{2,1,0:T(8,128)S(1)}, f32[16,16,128]{2,1,0:T(8,128)S(1)}, u32[]{:S(2)}, u32[]{:S(2)}) collective-permute-start(f32[16,16,128]{2,1,0:T(8,128)S(1)} %get-tuple-element.37), channel_id=1, source_target_pairs={{0,2},{1,3},{2,0},{3,1},{4,6},{5,7},{6,4},{7,5},{8,10},{9,11},{10,... | collective-permute-start | bytes 393224 | tf_op jit(solution)/shard_map/ppermute | solution.py:35
  44.5 1.3 %collective-permute-start.12 = (f32[16,16,128]{2,1,0:T(8,128)S(1)}, f32[16,16,128]{2,1,0:T(8,128)S(1)}, u32[]{:S(2)}, u32[]{:S(2)}) collective-permute-start(f32[16,16,128]{2,1,0:T(8,128)S(1)} %get-tuple-element.38), channel_id=1, source_target_pairs={{0,3},{1,2},{2,1},{3,0},{4,7},{5,6},{6,5},{7,4},{8,11},{9,10},{10,... | collective-permute-start | bytes 393224 | tf_op jit(solution)/shard_map/ppermute | solution.py:35
  45.8 4.2 %shard_map.61 = (f32[1024,512]{1,0:T(8,128)S(1)}, f32[8,4,64,128]{3,2,1,0:T(8,128)S(1)}, bf16[1024,512]{1,0:T(8,128)(2,1)S(1)}, bf16[1024,512]{1,0:T(8,128)(2,1)S(1)}) custom-call(bf16[1024,2048]{1,0:T(8,128)(2,1)} %refs_0_.7, bf16[2048,1024]{1,0:T(8,128)(2,1)S(1)} %get-tuple-element.39.refs_1_.refs_2_, bf16[1024,2048]{1,0:T(8,128)(2,1)S(1)} %get-tuple-element.40.refs_2_.refs_3_), custom_call_target="tpu_custom_call" | custom-call | flops 400000000 | bytes 8388608 | tf_op jit(solution)/shard_map/pallas_call | solution.py:156
  50.0 3.0 %shard_map.62 = (f32[1024,512]{1,0:T(8,128)S(1)}, f32[8,4,64,128]{3,2,1,0:T(8,128)S(1)}, bf16[1024,512]{1,0:T(8,128)(2,1)S(1)}) custom-call(bf16[1024,2048]{1,0:T(8,128)(2,1)} %refs_0_.7, bf16[1024,512]{1,0:T(8,128)(2,1)S(1)} %get-tuple-element.42.refs_1_.refs_13_, bf16[2048,1024]{1,0:T(8,128)(2,1)S(1)} %get-tuple-element.39.refs_1_.refs_2_, ...), custom_call_target="tpu_custom_call" | custom-call | flops 400000000 | bytes 8388608 | tf_op jit(solution)/shard_map/pallas_call | solution.py:156
  53.0 3.0 %shard_map.63 = (f32[1024,512]{1,0:T(8,128)S(1)}, f32[8,4,64,128]{3,2,1,0:T(8,128)S(1)}, bf16[1024,512]{1,0:T(8,128)(2,1)S(1)}) custom-call(bf16[1024,2048]{1,0:T(8,128)(2,1)} %refs_0_.7, bf16[1024,512]{1,0:T(8,128)(2,1)S(1)} %get-tuple-element.44.refs_1_.refs_14_, bf16[2048,1024]{1,0:T(8,128)(2,1)S(1)} %get-tuple-element.39.refs_1_.refs_2_, ...), custom_call_target="tpu_custom_call" | custom-call | flops 400000000 | bytes 8388608 | tf_op jit(solution)/shard_map/pallas_call | solution.py:156
  56.1 3.0 %shard_map.64 = (f32[1024,512]{1,0:T(8,128)S(1)}, f32[8,4,64,128]{3,2,1,0:T(8,128)S(1)}) custom-call(bf16[1024,2048]{1,0:T(8,128)(2,1)} %refs_0_.7, bf16[1024,512]{1,0:T(8,128)(2,1)S(1)} %get-tuple-element.46.refs_1_.refs_15_, bf16[2048,1024]{1,0:T(8,128)(2,1)S(1)} %get-tuple-element.39.refs_1_.refs_2_, bf16[1024,2048]{1,0:T(8,128)(2,1)S(1)} %get-tuple-element.40.refs_2_.refs_3_), custom_call_target="tpu_custom_call" | custom-call | flops 400000000 | bytes 8388608 | tf_op jit(solution)/shard_map/pallas_call | solution.py:156
  59.1 4.2 %output.1 = (bf16[1024,2048]{1,0:T(8,128)(2,1)}, f32[8,128]{1,0:T(8,128)}) custom-call(f32[16,16,128]{2,1,0:T(8,128)S(1)} %get-tuple-element.35.refs_0_, f32[16,16,128]{2,1,0:T(8,128)S(1)} %collective-permute-done.10.refs_1_, f32[16,16,128]{2,1,0:T(8,128)S(1)} %collective-permute-done.11.refs_2_, f32[16,16,128]{2,1,0:T(8,128)S(1)} %collective-permute-done.12.refs_3_, ...), custom_call_target="tpu_custom_call" | custom-call | tf_op jit(solution)/shard_map/output/pallas_call | solution.py:238
  (15 shorter events, 0.8 us)
Async XLA Ops:
  4.9 8.8 %collective-permute-start.2 = (f32[16,16,128]{2,1,0:T(8,128)S(1)}, f32[16,16,128]{2,1,0:T(8,128)S(1)}, u32[]{:S(2)}, u32[]{:S(2)}) collective-permute-start(f32[16,16,128]{2,1,0:T(8,128)S(1)} %get-tuple-element.57), channel_id=1, source_target_pairs={{0,3},{1,2},{2,1},{3,0},{4,7},{5,6},{6,5},{7,4},{8,11},{9,10},{10,... | collective-permute-start | bytes 393224 | tf_op jit(solution)/shard_map/ppermute | solution.py:35
  8.1 7.9 %collective-permute-start.1 = (f32[16,16,128]{2,1,0:T(8,128)S(1)}, f32[16,16,128]{2,1,0:T(8,128)S(1)}, u32[]{:S(2)}, u32[]{:S(2)}) collective-permute-start(f32[16,16,128]{2,1,0:T(8,128)S(1)} %get-tuple-element.58), channel_id=1, source_target_pairs={{0,2},{1,3},{2,0},{3,1},{4,6},{5,7},{6,4},{7,5},{8,10},{9,11},{10,... | collective-permute-start | bytes 393224 | tf_op jit(solution)/shard_map/ppermute | solution.py:35
  8.7 7.2 %collective-permute-start = (f32[16,16,128]{2,1,0:T(8,128)S(1)}, f32[16,16,128]{2,1,0:T(8,128)S(1)}, u32[]{:S(2)}, u32[]{:S(2)}) collective-permute-start(f32[16,16,128]{2,1,0:T(8,128)S(1)} %get-tuple-element.59), channel_id=1, source_target_pairs={{0,1},{1,0},{2,3},{3,2},{4,5},{5,4},{6,7},{7,6},{8,9},{9,8},{10,11... | collective-permute-start | bytes 393224 | tf_op jit(solution)/shard_map/ppermute | solution.py:35
  16.0 1.4 %collective-permute-start.3 = (f32[16,16,128]{2,1,0:T(8,128)S(1)}, f32[16,16,128]{2,1,0:T(8,128)S(1)}, u32[]{:S(2)}, u32[]{:S(2)}) collective-permute-start(f32[16,16,128]{2,1,0:T(8,128)S(1)} %add_add_fusion.row_ref), channel_id=1, source_target_pairs={{0,16},{1,17},{2,18},{3,19},{4,20},{5,21},{6,22},{7,23},{8,24},{9,... | collective-permute-start | bytes 393224 | tf_op jit(solution)/shard_map/ppermute | solution.py:35
  17.5 10.0 %collective-permute-start.6 = (f32[16,16,128]{2,1,0:T(8,128)S(1)}, f32[16,16,128]{2,1,0:T(8,128)S(1)}, u32[]{:S(2)}, u32[]{:S(2)}) collective-permute-start(f32[16,16,128]{2,1,0:T(8,128)S(1)} %add.15), channel_id=1, source_target_pairs={{0,96},{1,97},{2,98},{3,99},{4,100},{5,101},{6,102},{7,103},{8,104... | collective-permute-start | bytes 393224 | tf_op jit(solution)/shard_map/ppermute | solution.py:35
  21.6 7.9 %collective-permute-start.5 = (f32[16,16,128]{2,1,0:T(8,128)S(1)}, f32[16,16,128]{2,1,0:T(8,128)S(1)}, u32[]{:S(2)}, u32[]{:S(2)}) collective-permute-start(f32[16,16,128]{2,1,0:T(8,128)S(1)} %add.15), channel_id=1, source_target_pairs={{0,64},{1,65},{2,66},{3,67},{4,68},{5,69},{6,70},{7,71},{8,72},{9,... | collective-permute-start | bytes 393224 | tf_op jit(solution)/shard_map/ppermute | solution.py:35
  21.6 7.9 %collective-permute-start.4 = (f32[16,16,128]{2,1,0:T(8,128)S(1)}, f32[16,16,128]{2,1,0:T(8,128)S(1)}, u32[]{:S(2)}, u32[]{:S(2)}) collective-permute-start(f32[16,16,128]{2,1,0:T(8,128)S(1)} %add.15), channel_id=1, source_target_pairs={{0,32},{1,33},{2,34},{3,35},{4,36},{5,37},{6,38},{7,39},{8,40},{9,... | collective-permute-start | bytes 393224 | tf_op jit(solution)/shard_map/ppermute | solution.py:35
  29.5 6.5 %collective-permute-start.7 = (f32[17,16,128]{2,1,0:T(8,128)S(1)}, f32[17,16,128]{2,1,0:T(8,128)S(1)}, u32[]{:S(2)}, u32[]{:S(2)}) collective-permute-start(f32[17,16,128]{2,1,0:T(8,128)S(1)} %get-tuple-element.32), channel_id=1, source_target_pairs={{0,4},{1,5},{2,6},{3,7},{4,0},{5,1},{6,2},{7,3},{8,12},{9,13},{10,... | collective-permute-start | bytes 417800 | tf_op jit(solution)/shard_map/ppermute | solution.py:35
  31.1 8.1 %collective-permute-start.8 = (f32[17,16,128]{2,1,0:T(8,128)S(1)}, f32[17,16,128]{2,1,0:T(8,128)S(1)}, u32[]{:S(2)}, u32[]{:S(2)}) collective-permute-start(f32[17,16,128]{2,1,0:T(8,128)S(1)} %get-tuple-element.33), channel_id=1, source_target_pairs={{0,8},{1,9},{2,10},{3,11},{4,12},{5,13},{6,14},{7,15},{8,0},{9,1},... | collective-permute-start | bytes 417800 | tf_op jit(solution)/shard_map/ppermute | solution.py:35
  33.8 7.0 %collective-permute-start.9 = (f32[17,16,128]{2,1,0:T(8,128)S(1)}, f32[17,16,128]{2,1,0:T(8,128)S(1)}, u32[]{:S(2)}, u32[]{:S(2)}) collective-permute-start(f32[17,16,128]{2,1,0:T(8,128)S(1)} %get-tuple-element.34), channel_id=1, source_target_pairs={{0,12},{1,13},{2,14},{3,15},{4,8},{5,9},{6,10},{7,11},{8,4},{9,5},... | collective-permute-start | bytes 417800 | tf_op jit(solution)/shard_map/ppermute | solution.py:35
  41.0 18.1 %collective-permute-start.10 = (f32[16,16,128]{2,1,0:T(8,128)S(1)}, f32[16,16,128]{2,1,0:T(8,128)S(1)}, u32[]{:S(2)}, u32[]{:S(2)}) collective-permute-start(f32[16,16,128]{2,1,0:T(8,128)S(1)} %get-tuple-element.36), channel_id=1, source_target_pairs={{0,1},{1,0},{2,3},{3,2},{4,5},{5,4},{6,7},{7,6},{8,9},{9,8},{10,11... | collective-permute-start | bytes 393224 | tf_op jit(solution)/shard_map/ppermute | solution.py:35
  41.7 17.4 %collective-permute-start.11 = (f32[16,16,128]{2,1,0:T(8,128)S(1)}, f32[16,16,128]{2,1,0:T(8,128)S(1)}, u32[]{:S(2)}, u32[]{:S(2)}) collective-permute-start(f32[16,16,128]{2,1,0:T(8,128)S(1)} %get-tuple-element.37), channel_id=1, source_target_pairs={{0,2},{1,3},{2,0},{3,1},{4,6},{5,7},{6,4},{7,5},{8,10},{9,11},{10,... | collective-permute-start | bytes 393224 | tf_op jit(solution)/shard_map/ppermute | solution.py:35
  44.5 14.6 %collective-permute-start.12 = (f32[16,16,128]{2,1,0:T(8,128)S(1)}, f32[16,16,128]{2,1,0:T(8,128)S(1)}, u32[]{:S(2)}, u32[]{:S(2)}) collective-permute-start(f32[16,16,128]{2,1,0:T(8,128)S(1)} %get-tuple-element.38), channel_id=1, source_target_pairs={{0,3},{1,2},{2,1},{3,0},{4,7},{5,6},{6,5},{7,4},{8,11},{9,10},{10,... | collective-permute-start | bytes 393224 | tf_op jit(solution)/shard_map/ppermute | solution.py:35
  56.0 3.1 %copy-start = (f32[2048]{0:T(1024)S(1)}, f32[2048]{0:T(1024)}, u32[]{:S(2)}) copy-start(f32[2048]{0:T(1024)} %param.7) | copy-start | bytes 24580

commit v3 on v2

--- a/solution.py
+++ b/solution.py
@@ -257,50 +257,57 @@
     return jnp.where(condition, array, jnp.zeros_like(array))
 
 
-def plane_kernel(row_ref, core_ref, *refs):
+def line_kernel(row_ref, *refs):
+    _, core, x, _ = coordinates()
+    line, (before_ref, mine_ref, other_ref) = refs[:3], refs[3:]
+    before = jnp.zeros(row_ref.shape, jnp.float32)
+    for k in range(1, 4):
+        before = before + keep((x ^ k) < x, line[k - 1][...])
+    before_ref[...] = before
+    plane = (row_ref[...] + line[0][...]) + (line[1][...] + line[2][...])
+    for i in range(PAIRS // 4):
+        zero, one = plane[i * 4 : i * 4 + 2], plane[i * 4 + 2 : i * 4 + 4]
+        mine_ref[i * 2 : i * 2 + 2] = jnp.where(core == 0, zero, one)
+        other_ref[i * 2 : i * 2 + 2] = jnp.where(core == 0, one, zero)
+
+
+def column_kernel(mine_ref, got_ref, *refs):
     z, core, x, _ = coordinates()
-    column, (before_ref, final_ref, *send_refs) = refs[:3], refs[3:]
-    row_sum, other_core = row_ref[...], core_ref[...]
-    before = keep(core == 1, other_core)
+    column, (own_ref, send_ref, final_ref) = refs[:3], refs[3:]
+    mine, got = mine_ref[...], got_ref[...]
+    below = jnp.zeros_like(mine)
     for k in range(1, 4):
-        before = before + keep((z ^ k) < z, column[k - 1][...])
-    before_ref[...] = before
-
-    def final_pair(k):
-        p = (z * 2 + core) * 2 + (x ^ k) // 2
-        chip = row_ref[p] + core_ref[p]
-        return chip + (column[0][p] + column[1][p] + column[2][p])
-
-    final_ref[...] = final_pair(0)
-    for k in range(1, 4):
-        send_refs[k - 1][:PAIRS] = before + keep(x < (x ^ k), row_sum)
-        send_refs[k - 1][PAIRS] = final_pair(k)
-
-
-def prefix_kernel(before_ref, final_ref, *refs):
-    _, _, _, y = coordinates()
-    plane, ring, sums, final_out = refs[:3], refs[3:7], refs[7:11], refs[11]
-    rows_before = before_ref[...] + (
-        plane[0][:PAIRS] + plane[1][:PAIRS] + plane[2][:PAIRS]
-    )
+        below = below + keep((z ^ k) < z, column[k - 1][...])
+    own_ref[...] = below + keep(core == 1, got)
+    send_ref[...] = below + keep(core == 0, mine)
+    p = z * 2 + x // 2
+    chip = mine_ref[p] + got_ref[p]
+    final_ref[...] = chip + (column[0][p] + column[1][p] + column[2][p])
+
+
+def prefix_kernel(before_ref, own_ref, other_ref, *refs):
+    _, core, _, y = coordinates()
+    ring, sums, rows_before = refs[:4], refs[4:8], refs[8]
+    for i in range(PAIRS // 4):
+        for half, ref in ((core, own_ref), (1 - core, other_ref)):
+            pairs = pl.ds(i * 4 + half * 2, 2)
+            rows_before[pairs] = before_ref[pairs] + ref[i * 2 : i * 2 + 2]
     states = [r[...] for r in ring]
     for j in range(4):
-        shorter = rows_before
+        shorter = rows_before[...]
         for k in range(4):
             if k != j:
                 shorter = shorter + keep((y ^ k) < (y ^ j), states[k])
         sums[j][...] = shorter
-    final_out[...] = final_ref[...] + (
-        plane[0][PAIRS] + plane[1][PAIRS] + plane[2][PAIRS]
-    )
-
-
-def small_call(kernel, out_shapes, *args):
+
+
+def small_call(kernel, out_shapes, *args, scratch=()):
     return pl.pallas_call(
         kernel,
         out_shape=[jax.ShapeDtypeStruct(s, jnp.float32) for s in out_shapes],
         in_specs=[IN_VMEM] * len(args),
         out_specs=[IN_VMEM] * len(out_shapes),
+        scratch_shapes=scratch,
         compiler_params=pltpu.CompilerParams(vmem_limit_bytes=4 << 20),
     )(*args)
 
@@ -316,20 +323,23 @@
 
     ring = [total[0]] + [exchange(total[k], dy=k) for k in range(1, 4)]
     row_sum = (ring[0] + ring[1]) + (ring[2] + ring[3])
-    other_core = exchange(row_sum, dc=1)
-    chip_sum = row_sum + other_core
+    line = [exchange(row_sum, dx=k) for k in range(1, 4)]
+    quarter, half = (PAIRS, QROWS, LANES), (PAIRS // 2, QROWS, LANES)
+    before, mine, other = small_call(line_kernel, [quarter, half, half], row_sum, *line)
+    got = exchange(other, dc=1)
+    chip_sum = mine + got
     column = [exchange(chip_sum, dz=k) for k in range(1, 4)]
-    quarter = (PAIRS, QROWS, LANES)
-    pair = (QROWS, LANES)
-    before, final, *sends = small_call(
-        plane_kernel,
-        [quarter, pair] + [(PAIRS + 1, QROWS, LANES)] * 3,
-        row_sum,
-        other_core,
-        *column,
+    own, send, final = small_call(column_kernel, [half, half, (QROWS, LANES)], mine, got, *column)
+    others = exchange(send, dc=1)
+    sums = small_call(
+        prefix_kernel,
+        [quarter] * 4,
+        before,
+        own,
+        others,
+        *ring,
+        scratch=[pltpu.VMEM(quarter, jnp.float32)],
     )
-    plane = [exchange(sends[k - 1], dx=k) for k in range(1, 4)]
-    *sums, final = small_call(prefix_kernel, [quarter] * 4 + [pair], before, final, *plane, *ring)
     prefixes = [sums[0]] + [exchange(sums[k], dy=k) for k in range(1, 4)]
     mixed, final_state = output(
         prefixes, atts, befores, qs, final, norm_gain.reshape(1, WIDTH)

time: 63.6 us -> 61.3 us (0.964)
  the two profiles are of different devices: /device:TPU:0 before, /device:TPU:1 now
where the time goes in v3:
time: 61.3 us; the launch traced here: 61.2 us
  starting transfers between devices  22.1 us (36%)
  Pallas kernels  22 us (36%)
  waiting for transfers between devices  16.1 us (26%)
  between operations  0.91 us (1%)
    ppermute x14, starting transfers between devices, exchange(): lax.ppermute(array, AXES, [(rank, rank ^ turn) for rank in range(128)])  22.1 us
    ppermute x14, waiting for transfers between devices, exchange(): lax.ppermute(array, AXES, [(rank, rank ^ turn) for rank in range(128)])  16.1 us
    pallas_call x4, Pallas kernels, inside(): pl.pallas_call(functools.partial(inside_kernel, group), out_shape=(pltpu....  13.2 us
    pallas_call x1, Pallas kernels, output(): pl.pallas_call(output_kernel, out_shape=(jax.ShapeDtypeStruct((ROWS, WIDT...  4.25 us
    pallas_call x1, Pallas kernels, totals(): pl.pallas_call(totals_kernel, out_shape=(jax.ShapeDtypeStruct((QUARTERS,...  4.21 us
  transfers between devices with their start and end apart: 14, of which 8 were waited for; matrix products, arithmetic and copies ran while one was open for 0% of the time, Pallas kernels for 22%

profile of v3, /device:TPU:1, one launch (start us, length us, event | category | flops | bytes accessed | tf_op | source)
XLA Modules:
  0.0 61.2 jit_solution(10550904280094728258)
XLA Ops:
  0.6 4.2 %totals.1 = (f32[4,16,16,128]{3,2,1,0:T(8,128)S(1)}, bf16[2048,1024]{1,0:T(8,128)(2,1)S(1)}, bf16[1024,2048]{1,0:T(8,128)(2,1)S(1)}) custom-call(bf16[1024,2048]{1,0:T(8,128)(2,1)} %k_hbm.1, bf16[1024,2048]{1,0:T(8,128)(2,1)} %v_hbm.1), custom_call_target="tpu_custom_call" | custom-call | tf_op jit(solution)/shard_map/totals/pallas_call | solution.py:74
  4.9 3.6 %collective-permute-start.2 = (f32[16,16,128]{2,1,0:T(8,128)S(1)}, f32[16,16,128]{2,1,0:T(8,128)S(1)}, u32[]{:S(2)}, u32[]{:S(2)}) collective-permute-start(f32[16,16,128]{2,1,0:T(8,128)S(1)} %get-tuple-element.57), channel_id=1, source_target_pairs={{0,3},{1,2},{2,1},{3,0},{4,7},{5,6},{6,5},{7,4},{8,11},{9,10},{10,... | collective-permute-start | bytes 393224 | tf_op jit(solution)/shard_map/ppermute | solution.py:35
  9.2 4.8 %collective-permute-done.2.refs_3_ = f32[16,16,128]{2,1,0:T(8,128)S(1)} collective-permute-done((f32[16,16,128]{2,1,0:T(8,128)S(1)}, f32[16,16,128]{2,1,0:T(8,128)S(1)}, u32[]{:S(2)}, u32[]{:S(2)}) %collective-permute-start.2) | collective-permute-done | bytes 131104 | tf_op jit(solution)/shard_map/ppermute | solution.py:35
  14.0 1.0 %collective-permute-done.refs_1_ = f32[16,16,128]{2,1,0:T(8,128)S(1)} collective-permute-done((f32[16,16,128]{2,1,0:T(8,128)S(1)}, f32[16,16,128]{2,1,0:T(8,128)S(1)}, u32[]{:S(2)}, u32[]{:S(2)}) %collective-permute-start) | collective-permute-done | bytes 131104 | tf_op jit(solution)/shard_map/ppermute | solution.py:35
  15.0 2.4 %collective-permute-start.5 = (f32[16,16,128]{2,1,0:T(8,128)S(1)}, f32[16,16,128]{2,1,0:T(8,128)S(1)}, u32[]{:S(2)}, u32[]{:S(2)}) collective-permute-start(f32[16,16,128]{2,1,0:T(8,128)S(1)} %add_add_fusion.row_ref), channel_id=1, source_target_pairs={{0,12},{1,13},{2,14},{3,15},{4,8},{5,9},{6,10},{7,11},{8,4},{9,5},... | collective-permute-start | bytes 393224 | tf_op jit(solution)/shard_map/ppermute | solution.py:35
  17.5 0.5 collective-permute-start.4
  18.0 0.4 collective-permute-start.3
  18.4 2.4 %collective-permute-done.5.refs_2_ = f32[16,16,128]{2,1,0:T(8,128)S(1)} collective-permute-done((f32[16,16,128]{2,1,0:T(8,128)S(1)}, f32[16,16,128]{2,1,0:T(8,128)S(1)}, u32[]{:S(2)}, u32[]{:S(2)}) %collective-permute-start.5) | collective-permute-done | bytes 131104 | tf_op jit(solution)/shard_map/ppermute | solution.py:35
  20.8 2.1 %collective-permute-done.4.refs_1_ = f32[16,16,128]{2,1,0:T(8,128)S(1)} collective-permute-done((f32[16,16,128]{2,1,0:T(8,128)S(1)}, f32[16,16,128]{2,1,0:T(8,128)S(1)}, u32[]{:S(2)}, u32[]{:S(2)}) %collective-permute-start.4) | collective-permute-done | bytes 131104 | tf_op jit(solution)/shard_map/ppermute | solution.py:35
  23.0 3.9 %collective-permute-start.6 = (f32[8,16,128]{2,1,0:T(8,128)S(1)}, f32[8,16,128]{2,1,0:T(8,128)S(1)}, u32[]{:S(2)}, u32[]{:S(2)}) collective-permute-start(f32[8,16,128]{2,1,0:T(8,128)S(1)} %get-tuple-element.32), channel_id=1, source_target_pairs={{0,16},{1,17},{2,18},{3,19},{4,20},{5,21},{6,22},{7,23},{8,24},{9,... | collective-permute-start | bytes 196616 | tf_op jit(solution)/shard_map/ppermute | solution.py:35
  26.8 0.9 %collective-permute-done.6.got_ref = f32[8,16,128]{2,1,0:T(8,128)S(1)} collective-permute-done((f32[8,16,128]{2,1,0:T(8,128)S(1)}, f32[8,16,128]{2,1,0:T(8,128)S(1)}, u32[]{:S(2)}, u32[]{:S(2)}) %collective-permute-start.6) | collective-permute-done | bytes 65568 | tf_op jit(solution)/shard_map/ppermute | solution.py:35
  27.8 3.8 %collective-permute-start.9 = (f32[8,16,128]{2,1,0:T(8,128)S(1)}, f32[8,16,128]{2,1,0:T(8,128)S(1)}, u32[]{:S(2)}, u32[]{:S(2)}) collective-permute-start(f32[8,16,128]{2,1,0:T(8,128)S(1)} %add.15), channel_id=1, source_target_pairs={{0,96},{1,97},{2,98},{3,99},{4,100},{5,101},{6,102},{7,103},{8,104... | collective-permute-start | bytes 196616 | tf_op jit(solution)/shard_map/ppermute | solution.py:35
  31.6 0.7 %collective-permute-start.7 = (f32[8,16,128]{2,1,0:T(8,128)S(1)}, f32[8,16,128]{2,1,0:T(8,128)S(1)}, u32[]{:S(2)}, u32[]{:S(2)}) collective-permute-start(f32[8,16,128]{2,1,0:T(8,128)S(1)} %add.15), channel_id=1, source_target_pairs={{0,32},{1,33},{2,34},{3,35},{4,36},{5,37},{6,38},{7,39},{8,40},{9,... | collective-permute-start | bytes 196616 | tf_op jit(solution)/shard_map/ppermute | solution.py:35
  32.3 1.4 %collective-permute-done.9.refs_2_ = f32[8,16,128]{2,1,0:T(8,128)S(1)} collective-permute-done((f32[8,16,128]{2,1,0:T(8,128)S(1)}, f32[8,16,128]{2,1,0:T(8,128)S(1)}, u32[]{:S(2)}, u32[]{:S(2)}) %collective-permute-start.9) | collective-permute-done | bytes 65568 | tf_op jit(solution)/shard_map/ppermute | solution.py:35
  33.7 2.5 %collective-permute-done.8.refs_1_ = f32[8,16,128]{2,1,0:T(8,128)S(1)} collective-permute-done((f32[8,16,128]{2,1,0:T(8,128)S(1)}, f32[8,16,128]{2,1,0:T(8,128)S(1)}, u32[]{:S(2)}, u32[]{:S(2)}) %collective-permute-start.8) | collective-permute-done | bytes 65568 | tf_op jit(solution)/shard_map/ppermute | solution.py:35
  36.3 2.2 %collective-permute-start.10 = (f32[8,16,128]{2,1,0:T(8,128)S(1)}, f32[8,16,128]{2,1,0:T(8,128)S(1)}, u32[]{:S(2)}, u32[]{:S(2)}) collective-permute-start(f32[8,16,128]{2,1,0:T(8,128)S(1)} %get-tuple-element.34), channel_id=1, source_target_pairs={{0,16},{1,17},{2,18},{3,19},{4,20},{5,21},{6,22},{7,23},{8,24},{9,... | collective-permute-start | bytes 196616 | tf_op jit(solution)/shard_map/ppermute | solution.py:35
  38.4 0.9 %collective-permute-done.10.other_ref = f32[8,16,128]{2,1,0:T(8,128)S(1)} collective-permute-done((f32[8,16,128]{2,1,0:T(8,128)S(1)}, f32[8,16,128]{2,1,0:T(8,128)S(1)}, u32[]{:S(2)}, u32[]{:S(2)}) %collective-permute-start.10) | collective-permute-done | bytes 65568 | tf_op jit(solution)/shard_map/ppermute | solution.py:35
  39.5 0.7 %collective-permute-start.11 = (f32[16,16,128]{2,1,0:T(8,128)S(1)}, f32[16,16,128]{2,1,0:T(8,128)S(1)}, u32[]{:S(2)}, u32[]{:S(2)}) collective-permute-start(f32[16,16,128]{2,1,0:T(8,128)S(1)} %get-tuple-element.36), channel_id=1, source_target_pairs={{0,1},{1,0},{2,3},{3,2},{4,5},{5,4},{6,7},{7,6},{8,9},{9,8},{10,11... | collective-permute-start | bytes 393224 | tf_op jit(solution)/shard_map/ppermute | solution.py:35
  40.2 2.9 %collective-permute-start.12 = (f32[16,16,128]{2,1,0:T(8,128)S(1)}, f32[16,16,128]{2,1,0:T(8,128)S(1)}, u32[]{:S(2)}, u32[]{:S(2)}) collective-permute-start(f32[16,16,128]{2,1,0:T(8,128)S(1)} %get-tuple-element.37), channel_id=1, source_target_pairs={{0,2},{1,3},{2,0},{3,1},{4,6},{5,7},{6,4},{7,5},{8,10},{9,11},{10,... | collective-permute-start | bytes 393224 | tf_op jit(solution)/shard_map/ppermute | solution.py:35
  43.5 4.2 %shard_map.62 = (f32[1024,512]{1,0:T(8,128)S(1)}, f32[8,4,64,128]{3,2,1,0:T(8,128)S(1)}, bf16[1024,512]{1,0:T(8,128)(2,1)S(1)}, bf16[1024,512]{1,0:T(8,128)(2,1)S(1)}) custom-call(bf16[1024,2048]{1,0:T(8,128)(2,1)} %refs_0_.7, bf16[2048,1024]{1,0:T(8,128)(2,1)S(1)} %get-tuple-element.39.refs_1_.refs_2_, bf16[1024,2048]{1,0:T(8,128)(2,1)S(1)} %get-tuple-element.40.refs_2_.refs_3_), custom_call_target="tpu_custom_call" | custom-call | flops 400000000 | bytes 8388608 | tf_op jit(solution)/shard_map/pallas_call | solution.py:156
  47.7 3.0 %shard_map.63 = (f32[1024,512]{1,0:T(8,128)S(1)}, f32[8,4,64,128]{3,2,1,0:T(8,128)S(1)}, bf16[1024,512]{1,0:T(8,128)(2,1)S(1)}) custom-call(bf16[1024,2048]{1,0:T(8,128)(2,1)} %refs_0_.7, bf16[1024,512]{1,0:T(8,128)(2,1)S(1)} %get-tuple-element.42.refs_1_.refs_13_, bf16[2048,1024]{1,0:T(8,128)(2,1)S(1)} %get-tuple-element.39.refs_1_.refs_2_, ...), custom_call_target="tpu_custom_call" | custom-call | flops 400000000 | bytes 8388608 | tf_op jit(solution)/shard_map/pallas_call | solution.py:156
  50.7 3.0 %shard_map.64 = (f32[1024,512]{1,0:T(8,128)S(1)}, f32[8,4,64,128]{3,2,1,0:T(8,128)S(1)}, bf16[1024,512]{1,0:T(8,128)(2,1)S(1)}) custom-call(bf16[1024,2048]{1,0:T(8,128)(2,1)} %refs_0_.7, bf16[1024,512]{1,0:T(8,128)(2,1)S(1)} %get-tuple-element.44.refs_1_.refs_14_, bf16[2048,1024]{1,0:T(8,128)(2,1)S(1)} %get-tuple-element.39.refs_1_.refs_2_, ...), custom_call_target="tpu_custom_call" | custom-call | flops 400000000 | bytes 8388608 | tf_op jit(solution)/shard_map/pallas_call | solution.py:156
  53.7 3.0 %shard_map.65 = (f32[1024,512]{1,0:T(8,128)S(1)}, f32[8,4,64,128]{3,2,1,0:T(8,128)S(1)}) custom-call(bf16[1024,2048]{1,0:T(8,128)(2,1)} %refs_0_.7, bf16[1024,512]{1,0:T(8,128)(2,1)S(1)} %get-tuple-element.46.refs_1_.refs_15_, bf16[2048,1024]{1,0:T(8,128)(2,1)S(1)} %get-tuple-element.39.refs_1_.refs_2_, bf16[1024,2048]{1,0:T(8,128)(2,1)S(1)} %get-tuple-element.40.refs_2_.refs_3_), custom_call_target="tpu_custom_call" | custom-call | flops 400000000 | bytes 8388608 | tf_op jit(solution)/shard_map/pallas_call | solution.py:156
  56.8 4.2 %output.1 = (bf16[1024,2048]{1,0:T(8,128)(2,1)}, f32[8,128]{1,0:T(8,128)}) custom-call(f32[16,16,128]{2,1,0:T(8,128)S(1)} %get-tuple-element.35.refs_0_, f32[16,16,128]{2,1,0:T(8,128)S(1)} %collective-permute-done.11.refs_1_, f32[16,16,128]{2,1,0:T(8,128)S(1)} %collective-permute-done.12.refs_2_, f32[16,16,128]{2,1,0:T(8,128)S(1)} %collective-permute-done.13.refs_3_, ...), custom_call_target="tpu_custom_call" | custom-call | tf_op jit(solution)/shard_map/output/pallas_call | solution.py:238
  (18 shorter events, 1.4 us)
Async XLA Ops:
  4.9 9.1 %collective-permute-start.2 = (f32[16,16,128]{2,1,0:T(8,128)S(1)}, f32[16,16,128]{2,1,0:T(8,128)S(1)}, u32[]{:S(2)}, u32[]{:S(2)}) collective-permute-start(f32[16,16,128]{2,1,0:T(8,128)S(1)} %get-tuple-element.57), channel_id=1, source_target_pairs={{0,3},{1,2},{2,1},{3,0},{4,7},{5,6},{6,5},{7,4},{8,11},{9,10},{10,... | collective-permute-start | bytes 393224 | tf_op jit(solution)/shard_map/ppermute | solution.py:35
  8.5 5.5 %collective-permute-start.1 = (f32[16,16,128]{2,1,0:T(8,128)S(1)}, f32[16,16,128]{2,1,0:T(8,128)S(1)}, u32[]{:S(2)}, u32[]{:S(2)}) collective-permute-start(f32[16,16,128]{2,1,0:T(8,128)S(1)} %get-tuple-element.58), channel_id=1, source_target_pairs={{0,2},{1,3},{2,0},{3,1},{4,6},{5,7},{6,4},{7,5},{8,10},{9,11},{10,... | collective-permute-start | bytes 393224 | tf_op jit(solution)/shard_map/ppermute | solution.py:35
  8.9 6.1 %collective-permute-start = (f32[16,16,128]{2,1,0:T(8,128)S(1)}, f32[16,16,128]{2,1,0:T(8,128)S(1)}, u32[]{:S(2)}, u32[]{:S(2)}) collective-permute-start(f32[16,16,128]{2,1,0:T(8,128)S(1)} %get-tuple-element.59), channel_id=1, source_target_pairs={{0,1},{1,0},{2,3},{3,2},{4,5},{5,4},{6,7},{7,6},{8,9},{9,8},{10,11... | collective-permute-start | bytes 393224 | tf_op jit(solution)/shard_map/ppermute | solution.py:35
  15.0 5.8 %collective-permute-start.5 = (f32[16,16,128]{2,1,0:T(8,128)S(1)}, f32[16,16,128]{2,1,0:T(8,128)S(1)}, u32[]{:S(2)}, u32[]{:S(2)}) collective-permute-start(f32[16,16,128]{2,1,0:T(8,128)S(1)} %add_add_fusion.row_ref), channel_id=1, source_target_pairs={{0,12},{1,13},{2,14},{3,15},{4,8},{5,9},{6,10},{7,11},{8,4},{9,5},... | collective-permute-start | bytes 393224 | tf_op jit(solution)/shard_map/ppermute | solution.py:35
  17.5 5.4 %collective-permute-start.4 = (f32[16,16,128]{2,1,0:T(8,128)S(1)}, f32[16,16,128]{2,1,0:T(8,128)S(1)}, u32[]{:S(2)}, u32[]{:S(2)}) collective-permute-start(f32[16,16,128]{2,1,0:T(8,128)S(1)} %add_add_fusion.row_ref), channel_id=1, source_target_pairs={{0,8},{1,9},{2,10},{3,11},{4,12},{5,13},{6,14},{7,15},{8,0},{9,1},... | collective-permute-start | bytes 393224 | tf_op jit(solution)/shard_map/ppermute | solution.py:35
  18.0 4.9 %collective-permute-start.3 = (f32[16,16,128]{2,1,0:T(8,128)S(1)}, f32[16,16,128]{2,1,0:T(8,128)S(1)}, u32[]{:S(2)}, u32[]{:S(2)}) collective-permute-start(f32[16,16,128]{2,1,0:T(8,128)S(1)} %add_add_fusion.row_ref), channel_id=1, source_target_pairs={{0,4},{1,5},{2,6},{3,7},{4,0},{5,1},{6,2},{7,3},{8,12},{9,13},{10,... | collective-permute-start | bytes 393224 | tf_op jit(solution)/shard_map/ppermute | solution.py:35
  23.0 4.8 %collective-permute-start.6 = (f32[8,16,128]{2,1,0:T(8,128)S(1)}, f32[8,16,128]{2,1,0:T(8,128)S(1)}, u32[]{:S(2)}, u32[]{:S(2)}) collective-permute-start(f32[8,16,128]{2,1,0:T(8,128)S(1)} %get-tuple-element.32), channel_id=1, source_target_pairs={{0,16},{1,17},{2,18},{3,19},{4,20},{5,21},{6,22},{7,23},{8,24},{9,... | collective-permute-start | bytes 196616 | tf_op jit(solution)/shard_map/ppermute | solution.py:35
  27.8 6.0 %collective-permute-start.9 = (f32[8,16,128]{2,1,0:T(8,128)S(1)}, f32[8,16,128]{2,1,0:T(8,128)S(1)}, u32[]{:S(2)}, u32[]{:S(2)}) collective-permute-start(f32[8,16,128]{2,1,0:T(8,128)S(1)} %add.15), channel_id=1, source_target_pairs={{0,96},{1,97},{2,98},{3,99},{4,100},{5,101},{6,102},{7,103},{8,104... | collective-permute-start | bytes 196616 | tf_op jit(solution)/shard_map/ppermute | solution.py:35
  31.6 4.6 %collective-permute-start.8 = (f32[8,16,128]{2,1,0:T(8,128)S(1)}, f32[8,16,128]{2,1,0:T(8,128)S(1)}, u32[]{:S(2)}, u32[]{:S(2)}) collective-permute-start(f32[8,16,128]{2,1,0:T(8,128)S(1)} %add.15), channel_id=1, source_target_pairs={{0,64},{1,65},{2,66},{3,67},{4,68},{5,69},{6,70},{7,71},{8,72},{9,... | collective-permute-start | bytes 196616 | tf_op jit(solution)/shard_map/ppermute | solution.py:35
  31.6 4.6 %collective-permute-start.7 = (f32[8,16,128]{2,1,0:T(8,128)S(1)}, f32[8,16,128]{2,1,0:T(8,128)S(1)}, u32[]{:S(2)}, u32[]{:S(2)}) collective-permute-start(f32[8,16,128]{2,1,0:T(8,128)S(1)} %add.15), channel_id=1, source_target_pairs={{0,32},{1,33},{2,34},{3,35},{4,36},{5,37},{6,38},{7,39},{8,40},{9,... | collective-permute-start | bytes 196616 | tf_op jit(solution)/shard_map/ppermute | solution.py:35
  36.3 3.1 %collective-permute-start.10 = (f32[8,16,128]{2,1,0:T(8,128)S(1)}, f32[8,16,128]{2,1,0:T(8,128)S(1)}, u32[]{:S(2)}, u32[]{:S(2)}) collective-permute-start(f32[8,16,128]{2,1,0:T(8,128)S(1)} %get-tuple-element.34), channel_id=1, source_target_pairs={{0,16},{1,17},{2,18},{3,19},{4,20},{5,21},{6,22},{7,23},{8,24},{9,... | collective-permute-start | bytes 196616 | tf_op jit(solution)/shard_map/ppermute | solution.py:35
  39.5 17.2 %collective-permute-start.11 = (f32[16,16,128]{2,1,0:T(8,128)S(1)}, f32[16,16,128]{2,1,0:T(8,128)S(1)}, u32[]{:S(2)}, u32[]{:S(2)}) collective-permute-start(f32[16,16,128]{2,1,0:T(8,128)S(1)} %get-tuple-element.36), channel_id=1, source_target_pairs={{0,1},{1,0},{2,3},{3,2},{4,5},{5,4},{6,7},{7,6},{8,9},{9,8},{10,11... | collective-permute-start | bytes 393224 | tf_op jit(solution)/shard_map/ppermute | solution.py:35
  40.2 16.5 %collective-permute-start.12 = (f32[16,16,128]{2,1,0:T(8,128)S(1)}, f32[16,16,128]{2,1,0:T(8,128)S(1)}, u32[]{:S(2)}, u32[]{:S(2)}) collective-permute-start(f32[16,16,128]{2,1,0:T(8,128)S(1)} %get-tuple-element.37), channel_id=1, source_target_pairs={{0,2},{1,3},{2,0},{3,1},{4,6},{5,7},{6,4},{7,5},{8,10},{9,11},{10,... | collective-permute-start | bytes 393224 | tf_op jit(solution)/shard_map/ppermute | solution.py:35
  43.1 13.6 %collective-permute-start.13 = (f32[16,16,128]{2,1,0:T(8,128)S(1)}, f32[16,16,128]{2,1,0:T(8,128)S(1)}, u32[]{:S(2)}, u32[]{:S(2)}) collective-permute-start(f32[16,16,128]{2,1,0:T(8,128)S(1)} %get-tuple-element.38), channel_id=1, source_target_pairs={{0,3},{1,2},{2,1},{3,0},{4,7},{5,6},{6,5},{7,4},{8,11},{9,10},{10,... | collective-permute-start | bytes 393224 | tf_op jit(solution)/shard_map/ppermute | solution.py:35
  53.7 3.1 %copy-start = (f32[2048]{0:T(1024)S(1)}, f32[2048]{0:T(1024)}, u32[]{:S(2)}) copy-start(f32[2048]{0:T(1024)} %param.7) | copy-start | bytes 24580

commit v4 on v2

v4 whole, which is shorter than its diff:
```python
import functools

import jax
import jax.numpy as jnp
from jax import lax
from jax.experimental import pallas as pl
from jax.experimental.pallas import tpu as pltpu
from jax.sharding import PartitionSpec as P


HEADS = 32
DK = 64
BLOCK = 128
LANES = 128
PAIRS = 16
ROWS = 1024
BLOCKS = ROWS // BLOCK
GROUPS = 4
GROUP_PAIRS = PAIRS // GROUPS
GROUP_COLS = GROUP_PAIRS * LANES
STATE_ROWS = GROUP_PAIRS * DK
TURNS = (0, 2, 3, 1)
SHARE_ROWS = DK // 4
WIDTH = HEADS * DK
AXES = ("outer", "inner")
IN_VMEM = pl.BlockSpec(memory_space=pltpu.VMEM)


def coordinates():
    outer, inner = lax.axis_index("outer"), lax.axis_index("inner")
    return outer // 2, outer % 2, inner // 4, inner % 4


def exchange(array, dz=0, dc=0, dx=0, dy=0):
    turn = ((dz * 2 + dc) * 4 + dx) * 4 + dy
    return lax.ppermute(array, AXES, [(rank, rank ^ turn) for rank in range(128)])


def on_chip(array):
    return pltpu.with_memory_space_constraint(array, pltpu.VMEM)


def off_chip(array):
    return pltpu.with_memory_space_constraint(array, pltpu.HBM)


def totals_kernel(k_hbm, v_hbm, total_ref, kt_ref, v_ref, k_ref, sems):
    copies = []
    for i in range(GROUPS):
        cols = pl.ds(i * GROUP_COLS, GROUP_COLS)
        pair = (
            pltpu.make_async_copy(k_hbm.at[:, cols], k_ref.at[:, cols], sems.at[0, i]),
            pltpu.make_async_copy(v_hbm.at[:, cols], v_ref.at[:, cols], sems.at[1, i]),
        )
        for copy in pair:
            copy.start()
        copies.append(pair)
    _, _, _, y = coordinates()
    low = lax.broadcasted_iota(jnp.int32, (DK, LANES), 1) < DK
    for i in range(GROUPS):
        for copy in copies[i]:
            copy.wait()
        for j in range(GROUP_PAIRS):
            p = i * GROUP_PAIRS + j
            cols = pl.ds(p * LANES, LANES)
            keys = k_ref[:, cols].T
            kt_ref[cols, :] = keys
            full = jnp.dot(keys, v_ref[:, cols], preferred_element_type=jnp.float32)
            state = jnp.where(low, full[:DK], full[DK:])
            total_ref[y ^ i, j * DK : (j + 1) * DK] = state


def totals(keys, values):
    return pl.pallas_call(
        totals_kernel,
        out_shape=(
            jax.ShapeDtypeStruct((GROUPS, STATE_ROWS, LANES), jnp.float32),
            pltpu.VMEM((WIDTH, ROWS), jnp.bfloat16),
            pltpu.VMEM((ROWS, WIDTH), jnp.bfloat16),
        ),
        in_specs=[pl.BlockSpec(memory_space=pl.ANY)] * 2,
        out_specs=(IN_VMEM,) * 3,
        scratch_shapes=[
            pltpu.VMEM((ROWS, WIDTH), jnp.bfloat16),
            pltpu.SemaphoreType.DMA((2, GROUPS)),
        ],
        compiler_params=pltpu.CompilerParams(vmem_limit_bytes=16 << 20),
        name="totals",
    )(off_chip(keys), off_chip(values))


def beside(state):
    low = lax.broadcasted_iota(jnp.int32, state.shape, 1) < DK
    zero = jnp.zeros_like(state)
    return jnp.concatenate([jnp.where(low, state, zero), jnp.where(low, zero, state)], 0)


def inside_kernel(group, *refs):
    _, _, _, y = coordinates()
    start = pl.multiple_of((y ^ TURNS[group]) * GROUP_COLS, GROUP_COLS)
    if group == 0:
        q_hbm, kt_ref, v_ref, att_ref, before_ref, q_ref, mask_ref, sems = refs
        fetches = []
        for k in range(GROUPS):
            cols = pl.ds(pl.multiple_of((y ^ TURNS[k]) * GROUP_COLS, GROUP_COLS), GROUP_COLS)
            fetches.append(
                pltpu.make_async_copy(q_hbm.at[:, cols], q_ref.at[:, cols], sems.at[k])
            )
            fetches[k].start()
    else:
        q_ref, kt_ref, v_ref, att_ref, before_ref, mask_ref = refs
    row = lax.broadcasted_iota(jnp.int32, (BLOCK, 2 * BLOCK), 0)
    col = lax.broadcasted_iota(jnp.int32, (BLOCK, 2 * BLOCK), 1)
    mask_ref[...] = jnp.where((col % BLOCK) <= row, 1.0, 0.0).astype(jnp.bfloat16)
    half = jnp.zeros((DK, BLOCK), jnp.bfloat16)
    before = [jnp.zeros((DK, LANES), jnp.float32)] * GROUP_PAIRS
    if group == 0:
        fetches[0].wait()
    for b in range(BLOCKS):
        rows = pl.ds(b * BLOCK, BLOCK)
        last = b == BLOCKS - 1
        for j in range(GROUP_PAIRS):
            here = pl.ds(j * LANES, LANES)
            cols = pl.ds(pl.multiple_of(start + j * LANES, LANES), LANES)
            q, keys, values = q_ref[rows, cols], kt_ref[cols, rows], v_ref[rows, cols]
            first, second = keys[:DK], keys[DK:]
            k_both = jnp.concatenate(
                [
                    jnp.concatenate([first, half], 1),
                    jnp.concatenate([half, second], 1),
                ],
                0,
            )
            v_both = beside(values)
            scores = jnp.dot(q, k_both, preferred_element_type=jnp.float32)
            weights = scores.astype(jnp.bfloat16) * mask_ref[...]
            left = weights
            if not last:
                left = jnp.concatenate([weights, jnp.concatenate([first, second], 1)], 0)
            both = jnp.dot(left, v_both, preferred_element_type=jnp.float32)
            att_ref[rows, here] = both[:BLOCK]
            before_ref[b, j] = before[j]
            if not last:
                before[j] = before[j] + both[BLOCK:]
    if group == 0:
        for fetch in fetches[1:]:
            fetch.wait()


def inside(group, queries, keys, values):
    out_shape = [
        pltpu.VMEM((ROWS, GROUP_COLS), jnp.float32),
        pltpu.VMEM((BLOCKS, GROUP_PAIRS, DK, LANES), jnp.float32),
    ]
    scratch = [pltpu.VMEM((BLOCK, 2 * BLOCK), jnp.bfloat16)]
    first = group == 0
    if first:
        out_shape.append(pltpu.VMEM((ROWS, WIDTH), jnp.bfloat16))
        scratch.append(pltpu.SemaphoreType.DMA((GROUPS,)))
    return pl.pallas_call(
        functools.partial(inside_kernel, group),
        out_shape=out_shape,
        in_specs=[pl.BlockSpec(memory_space=pl.ANY) if first else IN_VMEM] + [IN_VMEM] * 2,
        out_specs=[IN_VMEM] * len(out_shape),
        scratch_shapes=scratch,
        compiler_params=pltpu.CompilerParams(vmem_limit_bytes=10 << 20),
        cost_estimate=pl.CostEstimate(
            flops=400_000_000, bytes_accessed=8 << 20, transcendentals=0
        ),
    )((off_chip if first else on_chip)(queries), on_chip(keys), on_chip(values))


def normed(start, att_ref, before_ref, q_ref, gain_ref, prefix_ref, stage_ref, ready):
    wide = 2 * LANES
    owner_row = lax.broadcasted_iota(jnp.int32, (wide, wide), 0) // DK
    owner_col = lax.broadcasted_iota(jnp.int32, (wide, wide), 1) // DK
    average = jnp.where(owner_row == owner_col, 1.0 / DK, 0.0).astype(jnp.bfloat16)
    nothing = jnp.zeros((LANES, LANES), jnp.bfloat16)
    for quad in range(GROUP_PAIRS // 2):
        whole = [prefix_ref[pl.ds((quad * 2 + j) * DK, DK)] for j in range(2)]
        here = pl.ds(quad * wide, wide)
        cols = pl.ds(pl.multiple_of(start + quad * wide, wide), wide)
        parts = []
        for b in range(BLOCKS):
            rows = pl.ds(b * BLOCK, BLOCK)
            pair, other = (
                beside((whole[j] + before_ref[b, quad * 2 + j]).astype(jnp.bfloat16))
                for j in range(2)
            )
            states = jnp.concatenate(
                [
                    jnp.concatenate([pair, nothing], 1),
                    jnp.concatenate([nothing, other], 1),
                ],
                0,
            )
            carried = jnp.dot(q_ref[rows, cols], states, preferred_element_type=jnp.float32)
            parts.append(att_ref[rows, here] + carried)
        attended = jnp.concatenate(parts, 0)
        mean = jnp.dot(
            (attended * attended).astype(jnp.bfloat16),
            average,
            preferred_element_type=jnp.float32,
        )
        scale = lax.rsqrt(mean + 1e-06) * gain_ref[:, cols]
        stage_ref[:, here] = (attended * scale).astype(jnp.bfloat16)
        ready(quad)


def columns(group):
    _, _, _, y = coordinates()
    return pl.multiple_of((y ^ TURNS[group]) * GROUP_COLS, GROUP_COLS)


def plain_output(group, att, before, q, gain, prefix, stage):
    normed(columns(group), att, before, q, gain, prefix, stage, lambda quad: None)


def copying_output(group, att, before, q, gain, prefix, last_stage, mixed, stage, sem):
    copy = pltpu.make_async_copy(
        last_stage, mixed.at[:, pl.ds(columns(group - 1), GROUP_COLS)], sem
    )
    copy.start()
    plain_output(group, att, before, q, gain, prefix, stage)
    copy.wait()


def last_output(att, before, q, gain, prefix, *refs):
    stages, (first, second, third, _), refs = refs[:2], refs[2:6], refs[6:]
    mixed, final_out, stage, share, sems = refs
    group = GROUPS - 1
    start = columns(group)
    copies = []
    for k in (1, 2):
        cols = pl.ds(columns(k), GROUP_COLS)
        copies.append(pltpu.make_async_copy(stages[k - 1], mixed.at[:, cols], sems.at[k - 1]))
        copies[-1].start()

    def ready(quad):
        wide = 2 * LANES
        cols = pl.ds(pl.multiple_of(start + quad * wide, wide), wide)
        copy = pltpu.make_async_copy(
            stage.at[:, pl.ds(quad * wide, wide)], mixed.at[:, cols], sems.at[2 + quad]
        )
        copy.start()
        copies.append(copy)

    z, _, x, y = coordinates()
    tail = pl.ds(STATE_ROWS, SHARE_ROWS)
    rows = jnp.zeros((SHARE_ROWS, LANES), jnp.float32)
    for k, ref in zip(TURNS, (first, second, third, prefix)):
        rows = jnp.where((y ^ k) == z, ref[tail], rows)
    share[...] = jnp.where(x % 2 == 0, rows, pltpu.roll(rows, DK, 1))
    lane = lax.broadcasted_iota(jnp.int32, (8, LANES), 1)
    even, odd = share[pl.ds(0, 8, stride=2)], share[pl.ds(1, 8, stride=2)]
    final = jnp.where(lane < DK, even, pltpu.roll(odd, DK, 1))
    final_out[...] = final * float(ROWS * 128) ** (-0.5)

    normed(start, att, before, q, gain, prefix, stage, ready)
    for copy in copies:
        copy.wait()


def output(group, att, before, q, gain, prefixes, stages, mixed):
    part = pltpu.VMEM((ROWS, GROUP_COLS), jnp.bfloat16)
    whole = pltpu.HBM((ROWS, WIDTH), jnp.bfloat16)
    in_hbm = pl.BlockSpec(memory_space=pl.ANY)
    args = [*map(on_chip, (att, before, q)), gain, prefixes[group]]
    in_specs = [IN_VMEM] * len(args)
    kernel = functools.partial(plain_output, group)
    out_shape, out_specs, scratch, aliases = [part], [IN_VMEM], [], {}
    if group == 1:
        kernel = functools.partial(copying_output, group)
        args.append(on_chip(stages[0]))
        in_specs.append(IN_VMEM)
        out_shape, out_specs = [whole, part], [in_hbm, IN_VMEM]
        scratch = [pltpu.SemaphoreType.DMA(())]
    elif group == GROUPS - 1:
        kernel = last_output
        args.extend([on_chip(stages[1]), on_chip(stages[2]), *prefixes[:group]])
        in_specs.extend([IN_VMEM] * (2 + group) + [in_hbm])
        aliases = {len(args): 0}
        args.append(off_chip(mixed))
        out_shape = [whole, jax.ShapeDtypeStruct((8, LANES), jnp.float32)]
        out_specs = [in_hbm, IN_VMEM]
        scratch = [
            part,
            pltpu.VMEM((SHARE_ROWS, LANES), jnp.float32),
            pltpu.SemaphoreType.DMA((2 + GROUP_PAIRS // 2,)),
        ]
    return pl.pallas_call(
        kernel,
        out_shape=out_shape,
        in_specs=in_specs,
        out_specs=out_specs,
        scratch_shapes=scratch,
        input_output_aliases=aliases,
        compiler_params=pltpu.CompilerParams(vmem_limit_bytes=10 << 20),
    )(*args)


def keep(condition, array):
    return jnp.where(condition, array, jnp.zeros_like(array))


def line_kernel(row_ref, *refs):
    _, _, x, _ = coordinates()
    line, (before_ref, plane_ref) = refs[:3], refs[3:]
    before = jnp.zeros(row_ref.shape, jnp.float32)
    for k in range(1, 4):
        before = before + keep((x ^ k) < x, line[k - 1][...])
    before_ref[...] = before
    plane_ref[...] = (row_ref[...] + line[0][...]) + (line[1][...] + line[2][...])


def prefix_kernel(before_ref, plane_ref, other_ref, *refs):
    z, core, x, y = coordinates()
    column, ring, sums = refs[:3], refs[3:7], refs[7:11]
    rows_before = before_ref[...] + keep(core == 1, other_ref[...])
    for k in range(1, 4):
        rows_before = rows_before + keep((z ^ k) < z, column[k - 1][...])
    states = [r[...] for r in ring]
    head = core * 4 + x
    for j in range(4):
        shorter = rows_before
        for k in range(4):
            if k != j:
                shorter = shorter + keep((y ^ k) < (y ^ j), states[k])
        sums[j][:STATE_ROWS] = shorter
        share = pl.multiple_of(head // 2 * DK + (y ^ j) * SHARE_ROWS, SHARE_ROWS)
        rows = pl.ds(share, SHARE_ROWS)
        chip = plane_ref[rows] + other_ref[rows]
        sums[j][STATE_ROWS:] = chip + (column[0][rows] + column[1][rows] + column[2][rows])


def small_call(kernel, out_shapes, *args):
    return pl.pallas_call(
        kernel,
        out_shape=[jax.ShapeDtypeStruct(s, jnp.float32) for s in out_shapes],
        in_specs=[IN_VMEM] * len(args),
        out_specs=[IN_VMEM] * len(out_shapes),
        compiler_params=pltpu.CompilerParams(vmem_limit_bytes=4 << 20),
    )(*args)


def steps(queries, key_rows, value_rows, norm_gain):
    total, keys, values = totals(key_rows, value_rows)
    atts, befores = [], []
    for g in range(GROUPS):
        attended, before, *fetched = inside(g, queries, keys, values)
        if g == 0:
            queries = fetched[0]
        atts.append(attended)
        befores.append(before)

    ring = [total[0]] + [exchange(total[k], dy=k) for k in range(1, 4)]
    row_sum = (ring[0] + ring[1]) + (ring[2] + ring[3])
    line = [exchange(row_sum, dx=k) for k in range(1, 4)]
    group = (STATE_ROWS, LANES)
    before, plane = small_call(line_kernel, [group, group], row_sum, *line)
    other = exchange(plane, dc=1)
    chip_sum = plane + other
    column = [exchange(chip_sum, dz=k) for k in range(1, 4)]
    sums = small_call(
        prefix_kernel, [(STATE_ROWS + SHARE_ROWS, LANES)] * 4, before, plane, other, *column, *ring
    )
    prefixes = [sums[0]] + [exchange(sums[k], dy=k) for k in TURNS[1:]]
    gain = norm_gain.reshape(1, WIDTH)
    stages, mixed = [], None
    for g in range(GROUPS):
        result = output(
            g, atts[g], befores[g], queries, gain, prefixes, stages, mixed
        )
        stages.append(result[-1])
        if g == 1:
            mixed = result[0]
    return (result[0], result[1].reshape(8 * LANES))


def solution(mesh):
    return jax.shard_map(
        steps,
        mesh=mesh,
        in_specs=(P(AXES, None), P(AXES, None), P(AXES, None), P()),
        out_specs=(P(AXES, None), P(AXES)),
        check_vma=False,
    )
```

time: 63.6 us -> 63.6 us (level)
  Pallas kernels: 21.9 us -> 23.9 us
  waiting for transfers between devices: 21.7 us -> 20.3 us
    pallas_call x6 -> x9, Pallas kernels: 21.7 us -> 23.7 us  [the longest x4 13.4 us: inside(): pl.pallas_call(functools.partial(inside_kernel, group), out_shape=out_sha...]
    ppermute x13, waiting for transfers between devices: 21.7 us -> 20.3 us  [exchange(): lax.ppermute(array, AXES, [(rank, rank ^ turn) for rank in range(128)])]
  transfers between devices with their start and end apart: 13 -> 13, of which waited for: 8 -> 7; matrix products, arithmetic and copies ran while one was open for 0% -> 0% of each run, Pallas kernels for 21% -> 27%
where the time goes in v4:
time: 63.6 us; the launch traced here: 63.5 us
  Pallas kernels  23.9 us (38%)
  waiting for transfers between devices  20.3 us (32%)
  starting transfers between devices  18.3 us (29%)
  between operations  0.93 us (1%)
    ppermute x13, waiting for transfers between devices, exchange(): lax.ppermute(array, AXES, [(rank, rank ^ turn) for rank in range(128)])  20.3 us
    ppermute x13, starting transfers between devices, exchange(): lax.ppermute(array, AXES, [(rank, rank ^ turn) for rank in range(128)])  18.3 us
    pallas_call x4, Pallas kernels, inside(): pl.pallas_call(functools.partial(inside_kernel, group), out_shape=out_sha...  13.4 us
    pallas_call x4, Pallas kernels, output(): pl.pallas_call(kernel, out_shape=out_shape, in_specs=in_specs, out_specs=...  6.08 us
    pallas_call x1, Pallas kernels, totals(): pl.pallas_call(totals_kernel, out_shape=(jax.ShapeDtypeStruct((GROUPS, ST...  4.2 us
  transfers between devices with their start and end apart: 13, of which 7 were waited for; matrix products, arithmetic and copies ran while one was open for 0% of the time, Pallas kernels for 27%

profile of v4, /device:TPU:0, one launch (start us, length us, event | category | flops | bytes accessed | tf_op | source)
XLA Modules:
  0.0 63.5 jit_solution(5748408288139995491)
XLA Ops:
  0.6 4.2 %totals.1 = (f32[4,256,128]{2,1,0:T(8,128)S(1)}, bf16[2048,1024]{1,0:T(8,128)(2,1)S(1)}, bf16[1024,2048]{1,0:T(8,128)(2,1)S(1)}) custom-call(bf16[1024,2048]{1,0:T(8,128)(2,1)} %k_hbm.1, bf16[1024,2048]{1,0:T(8,128)(2,1)} %v_hbm.1), custom_call_target="tpu_custom_call" | custom-call | tf_op jit(solution)/shard_map/totals/pallas_call | solution.py:74
  4.9 3.2 %collective-permute-start.2 = (f32[256,128]{1,0:T(8,128)S(1)}, f32[256,128]{1,0:T(8,128)S(1)}, u32[]{:S(2)}, u32[]{:S(2)}) collective-permute-start(f32[256,128]{1,0:T(8,128)S(1)} %get-tuple-element.47), channel_id=1, source_target_pairs={{0,3},{1,2},{2,1},{3,0},{4,7},{5,6},{6,5},{7,4},{8,11},{9,10},{10,... | collective-permute-start | bytes 393224 | tf_op jit(solution)/shard_map/ppermute | solution.py:36
  8.1 0.6 %collective-permute-start.1 = (f32[256,128]{1,0:T(8,128)S(1)}, f32[256,128]{1,0:T(8,128)S(1)}, u32[]{:S(2)}, u32[]{:S(2)}) collective-permute-start(f32[256,128]{1,0:T(8,128)S(1)} %get-tuple-element.48), channel_id=1, source_target_pairs={{0,2},{1,3},{2,0},{3,1},{4,6},{5,7},{6,4},{7,5},{8,10},{9,11},{10,... | collective-permute-start | bytes 393224 | tf_op jit(solution)/shard_map/ppermute | solution.py:36
  9.1 4.6 %collective-permute-done.2.refs_6_ = f32[256,128]{1,0:T(8,128)S(1)} collective-permute-done((f32[256,128]{1,0:T(8,128)S(1)}, f32[256,128]{1,0:T(8,128)S(1)}, u32[]{:S(2)}, u32[]{:S(2)}) %collective-permute-start.2) | collective-permute-done | bytes 131104 | tf_op jit(solution)/shard_map/ppermute | solution.py:36
  13.7 2.3 %collective-permute-done.1.refs_5_ = f32[256,128]{1,0:T(8,128)S(1)} collective-permute-done((f32[256,128]{1,0:T(8,128)S(1)}, f32[256,128]{1,0:T(8,128)S(1)}, u32[]{:S(2)}, u32[]{:S(2)}) %collective-permute-start.1) | collective-permute-done | bytes 131104 | tf_op jit(solution)/shard_map/ppermute | solution.py:36
  16.0 2.8 %collective-permute-start.5 = (f32[256,128]{1,0:T(8,128)S(1)}, f32[256,128]{1,0:T(8,128)S(1)}, u32[]{:S(2)}, u32[]{:S(2)}) collective-permute-start(f32[256,128]{1,0:T(8,128)S(1)} %add_add_fusion.row_ref), channel_id=1, source_target_pairs={{0,12},{1,13},{2,14},{3,15},{4,8},{5,9},{6,10},{7,11},{8,4},{9,5},... | collective-permute-start | bytes 393224 | tf_op jit(solution)/shard_map/ppermute | solution.py:36
  18.8 0.8 %collective-permute-start.4 = (f32[256,128]{1,0:T(8,128)S(1)}, f32[256,128]{1,0:T(8,128)S(1)}, u32[]{:S(2)}, u32[]{:S(2)}) collective-permute-start(f32[256,128]{1,0:T(8,128)S(1)} %add_add_fusion.row_ref), channel_id=1, source_target_pairs={{0,8},{1,9},{2,10},{3,11},{4,12},{5,13},{6,14},{7,15},{8,0},{9,1},... | collective-permute-start | bytes 393224 | tf_op jit(solution)/shard_map/ppermute | solution.py:36
  20.2 3.3 %collective-permute-done.5.refs_2_ = f32[256,128]{1,0:T(8,128)S(1)} collective-permute-done((f32[256,128]{1,0:T(8,128)S(1)}, f32[256,128]{1,0:T(8,128)S(1)}, u32[]{:S(2)}, u32[]{:S(2)}) %collective-permute-start.5) | collective-permute-done | bytes 131104 | tf_op jit(solution)/shard_map/ppermute | solution.py:36
  23.5 1.8 %collective-permute-done.4.refs_1_ = f32[256,128]{1,0:T(8,128)S(1)} collective-permute-done((f32[256,128]{1,0:T(8,128)S(1)}, f32[256,128]{1,0:T(8,128)S(1)}, u32[]{:S(2)}, u32[]{:S(2)}) %collective-permute-start.4) | collective-permute-done | bytes 131104 | tf_op jit(solution)/shard_map/ppermute | solution.py:36
  25.5 1.3 %collective-permute-done.6.other_ref = f32[256,128]{1,0:T(8,128)S(1)} collective-permute-done((f32[256,128]{1,0:T(8,128)S(1)}, f32[256,128]{1,0:T(8,128)S(1)}, u32[]{:S(2)}, u32[]{:S(2)}) %collective-permute-start.6) | collective-permute-done | bytes 131104 | tf_op jit(solution)/shard_map/ppermute | solution.py:36
  26.8 4.1 %collective-permute-start.9 = (f32[256,128]{1,0:T(8,128)S(1)}, f32[256,128]{1,0:T(8,128)S(1)}, u32[]{:S(2)}, u32[]{:S(2)}) collective-permute-start(f32[256,128]{1,0:T(8,128)S(1)} %add.15), channel_id=1, source_target_pairs={{0,96},{1,97},{2,98},{3,99},{4,100},{5,101},{6,102},{7,103},{8,104... | collective-permute-start | bytes 393224 | tf_op jit(solution)/shard_map/ppermute | solution.py:36
  30.9 0.9 %collective-permute-start.7 = (f32[256,128]{1,0:T(8,128)S(1)}, f32[256,128]{1,0:T(8,128)S(1)}, u32[]{:S(2)}, u32[]{:S(2)}) collective-permute-start(f32[256,128]{1,0:T(8,128)S(1)} %add.15), channel_id=1, source_target_pairs={{0,32},{1,33},{2,34},{3,35},{4,36},{5,37},{6,38},{7,39},{8,40},{9,... | collective-permute-start | bytes 393224 | tf_op jit(solution)/shard_map/ppermute | solution.py:36
  31.9 4.9 %collective-permute-done.9.refs_2_ = f32[256,128]{1,0:T(8,128)S(1)} collective-permute-done((f32[256,128]{1,0:T(8,128)S(1)}, f32[256,128]{1,0:T(8,128)S(1)}, u32[]{:S(2)}, u32[]{:S(2)}) %collective-permute-start.9) | collective-permute-done | bytes 131104 | tf_op jit(solution)/shard_map/ppermute | solution.py:36
  36.8 2.0 %collective-permute-done.8.refs_1_ = f32[256,128]{1,0:T(8,128)S(1)} collective-permute-done((f32[256,128]{1,0:T(8,128)S(1)}, f32[256,128]{1,0:T(8,128)S(1)}, u32[]{:S(2)}, u32[]{:S(2)}) %collective-permute-start.8) | collective-permute-done | bytes 131104 | tf_op jit(solution)/shard_map/ppermute | solution.py:36
  39.0 1.0 %collective-permute-start.10 = (f32[272,128]{1,0:T(8,128)S(1)}, f32[272,128]{1,0:T(8,128)S(1)}, u32[]{:S(2)}, u32[]{:S(2)}) collective-permute-start(f32[272,128]{1,0:T(8,128)S(1)} %get-tuple-element.32), channel_id=1, source_target_pairs={{0,1},{1,0},{2,3},{3,2},{4,5},{5,4},{6,7},{7,6},{8,9},{9,8},{10,11... | collective-permute-start | bytes 417800 | tf_op jit(solution)/shard_map/ppermute | solution.py:36
  40.0 3.2 %collective-permute-start.11 = (f32[272,128]{1,0:T(8,128)S(1)}, f32[272,128]{1,0:T(8,128)S(1)}, u32[]{:S(2)}, u32[]{:S(2)}) collective-permute-start(f32[272,128]{1,0:T(8,128)S(1)} %get-tuple-element.35), channel_id=1, source_target_pairs={{0,2},{1,3},{2,0},{3,1},{4,6},{5,7},{6,4},{7,5},{8,10},{9,11},{10,... | collective-permute-start | bytes 417800 | tf_op jit(solution)/shard_map/ppermute | solution.py:36
  43.7 4.3 %shard_map.59 = (f32[1024,512]{1,0:T(8,128)S(1)}, f32[8,4,64,128]{3,2,1,0:T(8,128)S(1)}, bf16[1024,2048]{1,0:T(8,128)(2,1)S(1)}) custom-call(bf16[1024,2048]{1,0:T(8,128)(2,1)} %refs_0_.1, bf16[2048,1024]{1,0:T(8,128)(2,1)S(1)} %get-tuple-element.24.refs_1_, bf16[1024,2048]{1,0:T(8,128)(2,1)S(1)} %get-tuple-element.25.refs_2_), custom_call_target="tpu_custom_call" | custom-call | flops 400000000 | bytes 8388608 | tf_op jit(solution)/shard_map/pallas_call | solution.py:160
  48.0 3.0 %shard_map.66 = (f32[1024,512]{1,0:T(8,128)S(1)}, f32[8,4,64,128]{3,2,1,0:T(8,128)S(1)}) custom-call(bf16[1024,2048]{1,0:T(8,128)(2,1)S(1)} %get-tuple-element.26.refs_0_.q, bf16[2048,1024]{1,0:T(8,128)(2,1)S(1)} %get-tuple-element.24.refs_1_, bf16[1024,2048]{1,0:T(8,128)(2,1)S(1)} %get-tuple-element.25.refs_2_), custom_call_target="tpu_custom_call" | custom-call | flops 400000000 | bytes 8388608 | tf_op jit(solution)/shard_map/pallas_call | solution.py:160
  51.1 3.0 %shard_map.63 = (f32[1024,512]{1,0:T(8,128)S(1)}, f32[8,4,64,128]{3,2,1,0:T(8,128)S(1)}) custom-call(bf16[1024,2048]{1,0:T(8,128)(2,1)S(1)} %get-tuple-element.26.refs_0_.q, bf16[2048,1024]{1,0:T(8,128)(2,1)S(1)} %get-tuple-element.24.refs_1_, bf16[1024,2048]{1,0:T(8,128)(2,1)S(1)} %get-tuple-element.25.refs_2_), custom_call_target="tpu_custom_call" | custom-call | flops 400000000 | bytes 8388608 | tf_op jit(solution)/shard_map/pallas_call | solution.py:160
  54.1 3.0 %shard_map.60 = (f32[1024,512]{1,0:T(8,128)S(1)}, f32[8,4,64,128]{3,2,1,0:T(8,128)S(1)}) custom-call(bf16[1024,2048]{1,0:T(8,128)(2,1)S(1)} %get-tuple-element.26.refs_0_.q, bf16[2048,1024]{1,0:T(8,128)(2,1)S(1)} %get-tuple-element.24.refs_1_, bf16[1024,2048]{1,0:T(8,128)(2,1)S(1)} %get-tuple-element.25.refs_2_), custom_call_target="tpu_custom_call" | custom-call | flops 400000000 | bytes 8388608 | tf_op jit(solution)/shard_map/pallas_call | solution.py:160
  57.2 0.9 %shard_map.64.last_stage = bf16[1024,512]{1,0:T(8,128)(2,1)S(1)} custom-call(f32[1024,512]{1,0:T(8,128)S(1)} %get-tuple-element.36.att, f32[8,4,64,128]{3,2,1,0:T(8,128)S(1)} %get-tuple-element.37.before, bf16[1024,2048]{1,0:T(8,128)(2,1)S(1)} %get-tuple-element.26.refs_0_.q, f32[1,2048]{1,0:T(1,128)S(1)} %bitcast.12, ...), custom_call_target="tpu_custom_call" | custom-call | tf_op jit(solution)/shard_map/pallas_call | solution.py:291
  58.2 1.0 %shard_map.67.refs_1_ = bf16[1024,512]{1,0:T(8,128)(2,1)S(1)} custom-call(f32[1024,512]{1,0:T(8,128)S(1)} %get-tuple-element.40.att, f32[8,4,64,128]{3,2,1,0:T(8,128)S(1)} %get-tuple-element.41.before, bf16[1024,2048]{1,0:T(8,128)(2,1)S(1)} %get-tuple-element.26.refs_0_.q, f32[1,2048]{1,0:T(1,128)S(1)} %bitcast.13, ...), custom_call_target="tpu_custom_call" | custom-call | tf_op jit(solution)/shard_map/pallas_call | solution.py:291
  59.2 1.7 %shard_map.65 = (bf16[1024,2048]{1,0:T(8,128)(2,1)}, bf16[1024,512]{1,0:T(8,128)(2,1)S(1)}) custom-call(f32[1024,512]{1,0:T(8,128)S(1)} %get-tuple-element.33.att, f32[8,4,64,128]{3,2,1,0:T(8,128)S(1)} %get-tuple-element.34.before, bf16[1024,2048]{1,0:T(8,128)(2,1)S(1)} %get-tuple-element.26.refs_0_.q, f32[1,2048]{1,0:T(1,128)S(1)} %bitcast.14, ...), custom_call_target="tpu_custom_call" | custom-call | tf_op jit(solution)/shard_map/pallas_call | solution.py:291
  60.8 2.5 %shard_map.68 = (bf16[1024,2048]{1,0:T(8,128)(2,1)}, f32[8,128]{1,0:T(8,128)}) custom-call(f32[1024,512]{1,0:T(8,128)S(1)} %get-tuple-element.27.att, f32[8,4,64,128]{3,2,1,0:T(8,128)S(1)} %get-tuple-element.28.before, bf16[1024,2048]{1,0:T(8,128)(2,1)S(1)} %get-tuple-element.26.refs_0_.q, f32[1,2048]{1,0:T(1,128)S(1)} %bitcast.15, ...), custom_call_target="tpu_custom_call", output_to_operand_aliasing={{0}: (10, {})} | custom-call | tf_op jit(solution)/shard_map/pallas_call | solution.py:291
  (18 shorter events, 1.9 us)
Async XLA Ops:
  4.9 8.8 %collective-permute-start.2 = (f32[256,128]{1,0:T(8,128)S(1)}, f32[256,128]{1,0:T(8,128)S(1)}, u32[]{:S(2)}, u32[]{:S(2)}) collective-permute-start(f32[256,128]{1,0:T(8,128)S(1)} %get-tuple-element.47), channel_id=1, source_target_pairs={{0,3},{1,2},{2,1},{3,0},{4,7},{5,6},{6,5},{7,4},{8,11},{9,10},{10,... | collective-permute-start | bytes 393224 | tf_op jit(solution)/shard_map/ppermute | solution.py:36
  8.1 7.9 %collective-permute-start.1 = (f32[256,128]{1,0:T(8,128)S(1)}, f32[256,128]{1,0:T(8,128)S(1)}, u32[]{:S(2)}, u32[]{:S(2)}) collective-permute-start(f32[256,128]{1,0:T(8,128)S(1)} %get-tuple-element.48), channel_id=1, source_target_pairs={{0,2},{1,3},{2,0},{3,1},{4,6},{5,7},{6,4},{7,5},{8,10},{9,11},{10,... | collective-permute-start | bytes 393224 | tf_op jit(solution)/shard_map/ppermute | solution.py:36
  8.7 7.2 %collective-permute-start = (f32[256,128]{1,0:T(8,128)S(1)}, f32[256,128]{1,0:T(8,128)S(1)}, u32[]{:S(2)}, u32[]{:S(2)}) collective-permute-start(f32[256,128]{1,0:T(8,128)S(1)} %get-tuple-element.49), channel_id=1, source_target_pairs={{0,1},{1,0},{2,3},{3,2},{4,5},{5,4},{6,7},{7,6},{8,9},{9,8},{10,11... | collective-permute-start | bytes 393224 | tf_op jit(solution)/shard_map/ppermute | solution.py:36
  16.0 7.5 %collective-permute-start.5 = (f32[256,128]{1,0:T(8,128)S(1)}, f32[256,128]{1,0:T(8,128)S(1)}, u32[]{:S(2)}, u32[]{:S(2)}) collective-permute-start(f32[256,128]{1,0:T(8,128)S(1)} %add_add_fusion.row_ref), channel_id=1, source_target_pairs={{0,12},{1,13},{2,14},{3,15},{4,8},{5,9},{6,10},{7,11},{8,4},{9,5},... | collective-permute-start | bytes 393224 | tf_op jit(solution)/shard_map/ppermute | solution.py:36
  18.8 6.5 %collective-permute-start.4 = (f32[256,128]{1,0:T(8,128)S(1)}, f32[256,128]{1,0:T(8,128)S(1)}, u32[]{:S(2)}, u32[]{:S(2)}) collective-permute-start(f32[256,128]{1,0:T(8,128)S(1)} %add_add_fusion.row_ref), channel_id=1, source_target_pairs={{0,8},{1,9},{2,10},{3,11},{4,12},{5,13},{6,14},{7,15},{8,0},{9,1},... | collective-permute-start | bytes 393224 | tf_op jit(solution)/shard_map/ppermute | solution.py:36
  19.6 5.7 %collective-permute-start.3 = (f32[256,128]{1,0:T(8,128)S(1)}, f32[256,128]{1,0:T(8,128)S(1)}, u32[]{:S(2)}, u32[]{:S(2)}) collective-permute-start(f32[256,128]{1,0:T(8,128)S(1)} %add_add_fusion.row_ref), channel_id=1, source_target_pairs={{0,4},{1,5},{2,6},{3,7},{4,0},{5,1},{6,2},{7,3},{8,12},{9,13},{10,... | collective-permute-start | bytes 393224 | tf_op jit(solution)/shard_map/ppermute | solution.py:36
  25.4 1.4 %collective-permute-start.6 = (f32[256,128]{1,0:T(8,128)S(1)}, f32[256,128]{1,0:T(8,128)S(1)}, u32[]{:S(2)}, u32[]{:S(2)}) collective-permute-start(f32[256,128]{1,0:T(8,128)S(1)} %get-tuple-element.31.plane_ref), channel_id=1, source_target_pairs={{0,16},{1,17},{2,18},{3,19},{4,20},{5,21},{6,22},{7,23},{8,24},{9,... | collective-permute-start | bytes 393224 | tf_op jit(solution)/shard_map/ppermute | solution.py:36
  26.8 10.0 %collective-permute-start.9 = (f32[256,128]{1,0:T(8,128)S(1)}, f32[256,128]{1,0:T(8,128)S(1)}, u32[]{:S(2)}, u32[]{:S(2)}) collective-permute-start(f32[256,128]{1,0:T(8,128)S(1)} %add.15), channel_id=1, source_target_pairs={{0,96},{1,97},{2,98},{3,99},{4,100},{5,101},{6,102},{7,103},{8,104... | collective-permute-start | bytes 393224 | tf_op jit(solution)/shard_map/ppermute | solution.py:36
  30.9 7.9 %collective-permute-start.8 = (f32[256,128]{1,0:T(8,128)S(1)}, f32[256,128]{1,0:T(8,128)S(1)}, u32[]{:S(2)}, u32[]{:S(2)}) collective-permute-start(f32[256,128]{1,0:T(8,128)S(1)} %add.15), channel_id=1, source_target_pairs={{0,64},{1,65},{2,66},{3,67},{4,68},{5,69},{6,70},{7,71},{8,72},{9,... | collective-permute-start | bytes 393224 | tf_op jit(solution)/shard_map/ppermute | solution.py:36
  30.9 7.9 %collective-permute-start.7 = (f32[256,128]{1,0:T(8,128)S(1)}, f32[256,128]{1,0:T(8,128)S(1)}, u32[]{:S(2)}, u32[]{:S(2)}) collective-permute-start(f32[256,128]{1,0:T(8,128)S(1)} %add.15), channel_id=1, source_target_pairs={{0,32},{1,33},{2,34},{3,35},{4,36},{5,37},{6,38},{7,39},{8,40},{9,... | collective-permute-start | bytes 393224 | tf_op jit(solution)/shard_map/ppermute | solution.py:36
  39.0 21.9 %collective-permute-start.10 = (f32[272,128]{1,0:T(8,128)S(1)}, f32[272,128]{1,0:T(8,128)S(1)}, u32[]{:S(2)}, u32[]{:S(2)}) collective-permute-start(f32[272,128]{1,0:T(8,128)S(1)} %get-tuple-element.32), channel_id=1, source_target_pairs={{0,1},{1,0},{2,3},{3,2},{4,5},{5,4},{6,7},{7,6},{8,9},{9,8},{10,11... | collective-permute-start | bytes 417800 | tf_op jit(solution)/shard_map/ppermute | solution.py:36
  40.0 19.2 %collective-permute-start.11 = (f32[272,128]{1,0:T(8,128)S(1)}, f32[272,128]{1,0:T(8,128)S(1)}, u32[]{:S(2)}, u32[]{:S(2)}) collective-permute-start(f32[272,128]{1,0:T(8,128)S(1)} %get-tuple-element.35), channel_id=1, source_target_pairs={{0,2},{1,3},{2,0},{3,1},{4,6},{5,7},{6,4},{7,5},{8,10},{9,11},{10,... | collective-permute-start | bytes 417800 | tf_op jit(solution)/shard_map/ppermute | solution.py:36
  43.1 15.0 %collective-permute-start.12 = (f32[272,128]{1,0:T(8,128)S(1)}, f32[272,128]{1,0:T(8,128)S(1)}, u32[]{:S(2)}, u32[]{:S(2)}) collective-permute-start(f32[272,128]{1,0:T(8,128)S(1)} %get-tuple-element.42), channel_id=1, source_target_pairs={{0,3},{1,2},{2,1},{3,0},{4,7},{5,6},{6,5},{7,4},{8,11},{9,10},{10,... | collective-permute-start | bytes 417800 | tf_op jit(solution)/shard_map/ppermute | solution.py:36
  54.1 3.1 %copy-start = (f32[2048]{0:T(1024)S(1)}, f32[2048]{0:T(1024)}, u32[]{:S(2)}) copy-start(f32[2048]{0:T(1024)} %param.7) | copy-start | bytes 24580
